TPU v7x, 256 devices: a whole 4x4x8 slice. The times are simulated.
256 devices in a mesh: gx: 8 (over z), gy: 8 (over y, core), gz: 4 (over x).
Axes of the slice: x: 4, y: 4, z: 8, core: 2. Of those that a mesh axis runs over, the one named last changes fastest.
Arguments:
- saved_heat_state: float32 [64, 128, 512], P('gx', 'gy', 'gz'), may hold values from 0 to 1
- forward_motion: float32 [3, 64, 128, 512], P(None, 'gx', 'gy', 'gz'), may hold values from -1 to 1
- dual_heat_after: float32 [64, 128, 512], P('gx', 'gy', 'gz'), may hold values from -1 to 6
- rheology_class: int32 [64, 128, 512], P('gx', 'gy', 'gz'), may hold values from 0 to 7, as said below
- class_base_stiffness: float32 [8], replicated, may hold values from 0.01 to 100
Outputs:
- adj_temp_prev: float32 [64, 128, 512], P('gx', 'gy', 'gz')
- adj_velocity: float32 [3, 64, 128, 512], P(None, 'gx', 'gy', 'gz')
- adj_pressure: float32 [64, 128, 512], P('gx', 'gy', 'gz')
Inputs may be any that keep to these rules, and one draw needn't show every extreme that they name: `rheology_class`: each cell's viscosity class.
All inputs are finite; a program needn't handle non-finite values.
Results may differ from a plain program's by a relative error of at most 0.0003.
Values sent between devices are 32-bit elements; how exact they have to be, the bound alone decides.
A program may use at most 128 MiB of HBM per device.

v0:
```python
import jax
import jax.numpy as jnp
from jax import lax
from jax.sharding import Mesh
from jax.sharding import PartitionSpec as P

RECOMPUTE = 2
SCHUR_ITERS = 4
COARSE_SWEEPS = 3
LAYERS = 8
GX_GY_GZ = ("gx", "gy_0", "gy_1", "gz")
GY = ("gy_0", "gy_1")


INCREMENT_DT = 0.2
DIFFUSIVITY = 0.3
ACTIVATION_ENERGY = 2.3
JACOBI_WEIGHT = 0.7
SCHUR_WEIGHT = 0.5
RAYLEIGH = 1.0


def extended(value, sides, width):
    edges = {}
    for axis, dim in sides:
        count, length = (lax.axis_size(axis), value.shape[dim])
        up = [(i, (i + 1) % count) for i in range(count - 1)]
        last = lax.slice_in_dim(value, length - width, length, axis=dim)
        initial = lax.slice_in_dim(value, 0, width, axis=dim)
        edges[dim] = (
            lax.ppermute(last, axis, up),
            lax.ppermute(initial, axis, [(b, a) for a, b in up]),
        )
    done = []
    for _, dim in sides:
        low, high = edges[dim]
        around = [(width, width) if d in done else (0, 0) for d in range(value.ndim)]
        value = jnp.concatenate([jnp.pad(low, around), value, jnp.pad(high, around)], axis=dim)
        done.append(dim)
    return value


def by_axis(value, axes):
    for axis in axes:
        value = lax.psum(value, axis)
    return value


def neighbours(bordered_array):
    centre = bordered_array[..., 1:-1, 1:-1, 1:-1]
    beside_all = [
        bordered_array[..., 2:, 1:-1, 1:-1],
        bordered_array[..., :-2, 1:-1, 1:-1],
        bordered_array[..., 1:-1, 2:, 1:-1],
        bordered_array[..., 1:-1, :-2, 1:-1],
        bordered_array[..., 1:-1, 1:-1, 2:],
        bordered_array[..., 1:-1, 1:-1, :-2],
    ]
    return (centre, beside_all)


def finest_halo_cells(field):
    return extended(field, (("gx", 1), (GY, 2), ("gz", 3)), 1)


def smooth_halo(field):
    return extended(field, (("gx", 1), (GY, 2), ("gz", 3)), 1)


def coarse_halo(field):
    return extended(field, (("gx", 1), (GY, 2), ("gz", 3)), 1)


def march_backward(bordered_array, shallower_adjacent, deeper_adjacent):
    centre, beside_all = neighbours(bordered_array)
    drift = 0.0
    for dim_index in range(3):
        drift = (
            drift
            + shallower_adjacent[dim_index] * (centre - beside_all[2 * dim_index + 1])
            + deeper_adjacent[dim_index] * (beside_all[2 * dim_index] - centre)
        )
    spread = sum(beside_all) - 6.0 * centre
    return centre - INCREMENT_DT * drift + INCREMENT_DT * DIFFUSIVITY * spread


def motion_source(bordered_heat, forward_motion, dual_heat_after):
    centre, beside_all = neighbours(bordered_heat)
    device_pieces = [
        jnp.where(
            forward_motion[dim_index] > 0,
            centre - beside_all[2 * dim_index + 1],
            beside_all[2 * dim_index] - centre,
        )
        for dim_index in range(3)
    ]
    return -INCREMENT_DT * dual_heat_after[None] * jnp.stack(device_pieces)


def advect_dual_heat(pos_padded, neg_padded, lam_padded):
    centre, beside_all = neighbours(lam_padded)
    result = centre + INCREMENT_DT * DIFFUSIVITY * (sum(beside_all) - 6.0 * centre)
    for dim_index in range(3):
        pos_centre, pos_around = neighbours(pos_padded[dim_index])
        neg_centre, neg_around = neighbours(neg_padded[dim_index])
        result = result - INCREMENT_DT * (
            pos_centre - pos_around[2 * dim_index] + neg_around[2 * dim_index + 1] - neg_centre
        )
    return result


def coefficients(bordered_array, factor):
    centre, beside_all = neighbours(bordered_array)
    return [factor * (0.5 * (centre + other)) for other in beside_all]


def apply_operator(face_coef, bordered_array):
    centre, beside_all = neighbours(bordered_array)
    return sum((coef * (centre - other) for coef, other in zip(face_coef, beside_all)))


def gradient(bordered_array):
    centre, beside_all = neighbours(bordered_array)
    return jnp.stack(
        [
            0.5 * (beside_all[2 * dim_index] - beside_all[2 * dim_index + 1])
            for dim_index in range(3)
        ]
    )


def divergence(bordered_array):
    centre, beside_all = neighbours(bordered_array)
    return sum(
        (
            0.5 * (beside_all[2 * dim_index][dim_index] - beside_all[2 * dim_index + 1][dim_index])
            for dim_index in range(3)
        )
    )


def restrict(field):
    leading = field.shape[:-3]
    cells_x, cells_y, cells_z = field.shape[-3:]
    blocks = field.reshape(leading + (cells_x // 2, 2, cells_y // 2, 2, cells_z // 2, 2))
    return blocks.mean(axis=(-5, -3, -1))


def prolong(field):
    return jnp.repeat(jnp.repeat(jnp.repeat(field, 2, axis=-3), 2, axis=-2), 2, axis=-1)


def evaluate_viscosity(rheology_class, class_base_stiffness):
    base = jnp.zeros(rheology_class.shape, jnp.float32)
    for layer_index in range(LAYERS):
        base = base + jnp.where(
            rheology_class == layer_index, class_base_stiffness[layer_index], 0.0
        )
    return base


def coarse_solve(coarse_res, coarse_coef, coarse_diag, pad_field):
    coarse_corr = JACOBI_WEIGHT * coarse_res / coarse_diag
    for sweep in range(COARSE_SWEEPS - 1):
        coarse_corr = (
            coarse_corr
            + JACOBI_WEIGHT
            * (coarse_res - apply_operator(coarse_coef, pad_field(coarse_corr)))
            / coarse_diag
        )
    return coarse_corr


def shards(saved_heat_state, forward_motion, dual_heat_after, rheology_class, class_base_stiffness):
    extent_first, extent_second, extent_vertical = saved_heat_state.shape
    shallower_adjacent = jnp.maximum(forward_motion, 0.0)
    deeper_adjacent = jnp.minimum(forward_motion, 0.0)
    heat_state = saved_heat_state
    for repeat_index in range(RECOMPUTE):
        heat_state = march_backward(
            finest_halo_cells(heat_state[None])[0], shallower_adjacent, deeper_adjacent
        )
    local_viscosity = evaluate_viscosity(rheology_class, class_base_stiffness) * jnp.exp(
        -ACTIVATION_ENERGY * heat_state
    )
    stacked = jnp.concatenate(
        [
            heat_state[None],
            dual_heat_after[None],
            shallower_adjacent * dual_heat_after[None],
            deeper_adjacent * dual_heat_after[None],
            local_viscosity[None],
        ],
        0,
    )
    bordered_array = finest_halo_cells(stacked)
    driving_source = motion_source(bordered_array[0], forward_motion, dual_heat_after)
    advected_result = advect_dual_heat(bordered_array[2:5], bordered_array[5:8], bordered_array[1])
    face_coef = coefficients(bordered_array[8], 1.0)
    diagonal = sum(face_coef)
    coarse_visc = restrict(local_viscosity)
    coarse_coef = coefficients(coarse_halo(coarse_visc[None])[0], 0.25)
    coarse_diag = sum(coarse_coef)
    total_cells = (
        extent_first
        * extent_second
        * extent_vertical
        * lax.axis_size("gx")
        * lax.axis_size(GY)
        * lax.axis_size("gz")
    )
    velocity = jnp.zeros(forward_motion.shape, jnp.float32)
    mean_stress = jnp.zeros(saved_heat_state.shape, jnp.float32)
    for iteration in range(SCHUR_ITERS):
        if iteration == 0:
            residual = driving_source
        else:
            flow_press = smooth_halo(jnp.concatenate([velocity, mean_stress[None]], 0))
            residual = (
                driving_source
                - apply_operator(face_coef, flow_press[0:3])
                - gradient(flow_press[3])
            )
        correction = JACOBI_WEIGHT * residual / diagonal
        residual_two = residual - apply_operator(face_coef, smooth_halo(correction))
        coarse_res = restrict(residual_two)
        coarse_corr = coarse_solve(coarse_res, coarse_coef, coarse_diag, coarse_halo)
        correction = correction + prolong(coarse_corr)
        correction = (
            correction
            + JACOBI_WEIGHT
            * (residual - apply_operator(face_coef, finest_halo_cells(correction)))
            / diagonal
        )
        velocity = velocity + correction
        spread_flow = divergence(finest_halo_cells(velocity))
        mean_stress = mean_stress - SCHUR_WEIGHT * local_viscosity * spread_flow
        mean_stress = mean_stress - by_axis(jnp.sum(mean_stress), GX_GY_GZ) / total_cells
    adj_temp_prev = advected_result + RAYLEIGH * velocity[2]
    return (adj_temp_prev, velocity, mean_stress)


def solution(mesh):
    split = Mesh(
        mesh.devices.reshape(mesh.shape["gx"], 4, 2, mesh.shape["gz"]), ("gx", "gy_0", "gy_1", "gz")
    )
    in_specs = (
        P("gx", GY, "gz"),
        P(None, "gx", GY, "gz"),
        P("gx", GY, "gz"),
        P("gx", GY, "gz"),
        P(),
    )
    out_specs = (P("gx", GY, "gz"), P(None, "gx", GY, "gz"), P("gx", GY, "gz"))
    return jax.shard_map(
        shards, mesh=split, in_specs=in_specs, out_specs=out_specs, check_vma=False
    )
```

profile of v0, /device:TPU:1, one launch (start us, length us, event | category | flops | bytes accessed | tf_op | source)
XLA Modules:
  0.0 884.7 jit_solution(9574616667842315440)
XLA Ops:
  27.2 5.6 collective-permute-start.7
  51.2 5.5 reshape.118
  107.4 5.5 collective-permute-start.19
  124.2 13.9 %reshape.117 = f32[3,4,2,8,2,64,2]{6,5,4,3,2,1,0:T(8,128)} reshape(f32[3,8,16,128]{3,2,1,0:T(8,128)S(1)} %fusion.253) | data formatting | bytes 393216 | tf_op jit(solution)/shard_map/reshape | solution.py:145
  138.1 5.5 reduce_sum.81
  149.8 5.5 collective-permute-start.31
  170.8 5.5 collective-permute-start.37
  233.4 18.4 %psum.112 = f32[]{:T(128)} all-reduce(f32[]{:T(128)} %get-tuple-element.36), channel_id=1, replica_groups=mesh['gx'=8,'gy_0'=4,'gy_1'=2,'gz'=4] {'gx'}, use_global_device_ids=true, to_apply=%region_3.4 | all-reduce | flops 1 | bytes 8 | tf_op jit(solution)/shard_map/psum | solution.py:45
  251.8 8.0 psum.113
  259.9 9.6 %psum.114 = f32[]{:T(128)} all-reduce(f32[]{:T(128)} %psum.113), channel_id=1, replica_groups=mesh['gx'=8,'gy_0'=4,'gy_1'=2,'gz'=4] {'gy_1'}, use_global_device_ids=true, to_apply=%region_5.6 | all-reduce | flops 1 | bytes 8 | tf_op jit(solution)/shard_map/psum | solution.py:45
  269.5 11.1 %psum.115 = f32[]{:T(128)} all-reduce(f32[]{:T(128)} %psum.114), channel_id=1, replica_groups=mesh['gx'=8,'gy_0'=4,'gy_1'=2,'gz'=4] {'gz'}, use_global_device_ids=true, to_apply=%region_6.7 | all-reduce | flops 1 | bytes 8 | tf_op jit(solution)/shard_map/psum | solution.py:45
  300.1 8.1 collective-permute-done.58
  331.1 13.9 %reshape.122 = f32[3,4,2,8,2,64,2]{6,5,4,3,2,1,0:T(8,128)} reshape(f32[3,8,16,128]{3,2,1,0:T(8,128)S(1)} %fusion.191) | data formatting | bytes 393216 | tf_op jit(solution)/shard_map/reshape | solution.py:145
  345.0 5.5 reduce_sum.84
  437.2 18.2 %psum.116 = f32[]{:T(128)} all-reduce(f32[]{:T(128)} %get-tuple-element.32), channel_id=1, replica_groups=mesh['gx'=8,'gy_0'=4,'gy_1'=2,'gz'=4] {'gx'}, use_global_device_ids=true, to_apply=%region_9.10 | all-reduce | flops 1 | bytes 8 | tf_op jit(solution)/shard_map/psum | solution.py:45
  455.4 6.6 psum.117
  462.0 10.0 %psum.118 = f32[]{:T(128)} all-reduce(f32[]{:T(128)} %psum.117), channel_id=1, replica_groups=mesh['gx'=8,'gy_0'=4,'gy_1'=2,'gz'=4] {'gy_1'}, use_global_device_ids=true, to_apply=%region_11.12 | all-reduce | flops 1 | bytes 8 | tf_op jit(solution)/shard_map/psum | solution.py:45
  472.0 11.3 %psum.119 = f32[]{:T(128)} all-reduce(f32[]{:T(128)} %psum.118), channel_id=1, replica_groups=mesh['gx'=8,'gy_0'=4,'gy_1'=2,'gz'=4] {'gz'}, use_global_device_ids=true, to_apply=%region_12.13 | all-reduce | flops 1 | bytes 8 | tf_op jit(solution)/shard_map/psum | solution.py:45
  502.8 8.1 collective-permute-done.94
  532.3 13.9 %reshape.126 = f32[3,4,2,8,2,64,2]{6,5,4,3,2,1,0:T(8,128)} reshape(f32[3,8,16,128]{3,2,1,0:T(8,128)S(1)} %fusion.128) | data formatting | bytes 393216 | tf_op jit(solution)/shard_map/reshape | solution.py:145
  546.3 5.5 reduce_sum.86
  637.7 18.2 %psum.120 = f32[]{:T(128)} all-reduce(f32[]{:T(128)} %get-tuple-element.28), channel_id=1, replica_groups=mesh['gx'=8,'gy_0'=4,'gy_1'=2,'gz'=4] {'gx'}, use_global_device_ids=true, to_apply=%region_15.16 | all-reduce | flops 1 | bytes 8 | tf_op jit(solution)/shard_map/psum | solution.py:45
  655.8 6.6 psum.121
  662.4 10.0 %psum.122 = f32[]{:T(128)} all-reduce(f32[]{:T(128)} %psum.121), channel_id=1, replica_groups=mesh['gx'=8,'gy_0'=4,'gy_1'=2,'gz'=4] {'gy_1'}, use_global_device_ids=true, to_apply=%region_17.18 | all-reduce | flops 1 | bytes 8 | tf_op jit(solution)/shard_map/psum | solution.py:45
  672.5 11.1 %psum.123 = f32[]{:T(128)} all-reduce(f32[]{:T(128)} %psum.122), channel_id=1, replica_groups=mesh['gx'=8,'gy_0'=4,'gy_1'=2,'gz'=4] {'gz'}, use_global_device_ids=true, to_apply=%region_18.19 | all-reduce | flops 1 | bytes 8 | tf_op jit(solution)/shard_map/psum | solution.py:45
  703.1 8.1 collective-permute-done.130
  732.6 13.9 %reshape.130 = f32[3,4,2,8,2,64,2]{6,5,4,3,2,1,0:T(8,128)} reshape(f32[3,8,16,128]{3,2,1,0:T(8,128)S(1)} %fusion.65) | data formatting | bytes 393216 | tf_op jit(solution)/shard_map/reshape | solution.py:145
  746.6 5.5 reduce_sum.88
  836.2 18.2 %psum.124 = f32[]{:T(128)} all-reduce(f32[]{:T(128)} %get-tuple-element.24), channel_id=1, replica_groups=mesh['gx'=8,'gy_0'=4,'gy_1'=2,'gz'=4] {'gx'}, use_global_device_ids=true, to_apply=%region_21.22 | all-reduce | flops 1 | bytes 8 | tf_op jit(solution)/shard_map/psum | solution.py:45
  854.4 6.6 psum.125
  861.0 10.0 %psum.126 = f32[]{:T(128)} all-reduce(f32[]{:T(128)} %psum.125), channel_id=1, replica_groups=mesh['gx'=8,'gy_0'=4,'gy_1'=2,'gz'=4] {'gy_1'}, use_global_device_ids=true, to_apply=%region_23.24 | all-reduce | flops 1 | bytes 8 | tf_op jit(solution)/shard_map/psum | solution.py:45
  872.0 11.1 %psum.127 = f32[]{:T(128)} all-reduce(f32[]{:T(128)} %psum.126), channel_id=1, replica_groups=mesh['gx'=8,'gy_0'=4,'gy_1'=2,'gz'=4] {'gz'}, use_global_device_ids=true, to_apply=%region_24.25 | all-reduce | flops 1 | bytes 8 | tf_op jit(solution)/shard_map/psum | solution.py:45
  (625 shorter events, 562.8 us)
Async XLA Ops:
  1.5 21.2 %collective-permute-start.1 = (f32[1,8,1,128]{3,2,1,0:T(1,128)S(1)}, f32[1,8,1,128]{3,2,1,0:T(1,128)S(1)}, u32[]{:S(2)}, u32[]{:S(2)}) collective-permute-start(f32[1,8,1,128]{3,2,1,0:T(1,128)S(1)} %get-tuple-element.185), channel_id=1, source_target_pairs={{0,4},{4,8},{8,12},{12,16},{16,20},{20,24},{24,28},{1,5},{5,9},{9,... | collective-permute-start | bytes 12296 | tf_op jit(solution)/shard_map/ppermute | solution.py:31
  6.1 16.6 %collective-permute-start.4 = (f32[1,8,1,128]{3,2,1,0:T(1,128)S(1)}, f32[1,8,1,128]{3,2,1,0:T(1,128)S(1)}, u32[]{:S(2)}, u32[]{:S(2)}) collective-permute-start(f32[1,8,1,128]{3,2,1,0:T(1,128)S(1)} %get-tuple-element.186), channel_id=1, source_target_pairs={{4,0},{8,4},{12,8},{16,12},{20,16},{24,20},{28,24},{5,1},{9,5},{13... | collective-permute-start | bytes 12296 | tf_op jit(solution)/shard_map/ppermute | solution.py:32
  24.0 16.3 %collective-permute-start.6 = (f32[1,8,16,1]{3,2,1,0:T(8,128)S(1)}, f32[1,8,16,1]{3,2,1,0:T(8,128)S(1)}, u32[]{:S(2)}, u32[]{:S(2)}) collective-permute-start(f32[1,8,16,1]{3,2,1,0:T(8,128)S(1)} %get-tuple-element.177), channel_id=1, source_target_pairs={{0,1},{1,2},{2,3},{4,5},{5,6},{6,7},{8,9},{9,10},{10,11},{12,13},{... | collective-permute-start | bytes 1544 | tf_op jit(solution)/shard_map/ppermute | solution.py:31
  27.2 18.2 %collective-permute-start.7 = (f32[1,8,1,128]{3,2,1,0:T(1,128)S(1)}, f32[1,8,1,128]{3,2,1,0:T(1,128)S(1)}, u32[]{:S(2)}, u32[]{:S(2)}) collective-permute-start(f32[1,8,1,128]{3,2,1,0:T(1,128)S(1)} %get-tuple-element.179), channel_id=1, source_target_pairs={{0,4},{4,8},{8,12},{12,16},{16,20},{20,24},{24,28},{1,5},{5,9},{9,... | collective-permute-start | bytes 12296 | tf_op jit(solution)/shard_map/ppermute | solution.py:31
  59.8 32.0 %collective-permute-start.12 = (f32[9,8,16,1]{2,1,3,0:T(8,128)S(1)}, f32[9,8,16,1]{2,1,3,0:T(8,128)S(1)}, u32[]{:S(2)}, u32[]{:S(2)}) collective-permute-start(f32[9,8,16,1]{2,1,3,0:T(8,128)S(1)} %copy.1935), channel_id=1, source_target_pairs={{0,1},{1,2},{2,3},{4,5},{5,6},{6,7},{8,9},{9,10},{10,11},{12,13},{... | collective-permute-start | bytes 13832 | tf_op jit(solution)/shard_map/ppermute | solution.py:31
  62.7 16.3 %collective-permute-start.25 = (f32[1,4,1,64]{3,2,1,0:T(1,128)S(1)}, f32[1,4,1,64]{3,2,1,0:T(1,128)S(1)}, u32[]{:S(2)}, u32[]{:S(2)}) collective-permute-start(f32[1,4,1,64]{3,2,1,0:T(1,128)S(1)} %get-tuple-element.239), channel_id=1, source_target_pairs={{0,4},{4,8},{8,12},{12,16},{16,20},{20,24},{24,28},{1,5},{5,9},{9,... | collective-permute-start | bytes 3080 | tf_op jit(solution)/shard_map/ppermute | solution.py:31
  79.0 18.8 %collective-permute-start.16 = (f32[9,8,1,128]{3,1,2,0:T(8,128)S(1)}, f32[9,8,1,128]{3,1,2,0:T(8,128)S(1)}, u32[]{:S(2)}, u32[]{:S(2)}) collective-permute-start(f32[9,8,1,128]{3,1,2,0:T(8,128)S(1)} %bitcast.266), channel_id=1, source_target_pairs={{4,0},{8,4},{12,8},{16,12},{20,16},{24,20},{28,24},{5,1},{9,5},{13... | collective-permute-start | bytes 110600 | tf_op jit(solution)/shard_map/ppermute | solution.py:32
  81.0 16.9 %collective-permute-start.13 = (f32[9,8,1,128]{3,1,2,0:T(8,128)S(1)}, f32[9,8,1,128]{3,1,2,0:T(8,128)S(1)}, u32[]{:S(2)}, u32[]{:S(2)}) collective-permute-start(f32[9,8,1,128]{3,1,2,0:T(8,128)S(1)} %bitcast.265), channel_id=1, source_target_pairs={{0,4},{4,8},{8,12},{12,16},{16,20},{20,24},{24,28},{1,5},{5,9},{9,... | collective-permute-start | bytes 110600 | tf_op jit(solution)/shard_map/ppermute | solution.py:31
  103.7 16.5 %collective-permute-start.21 = (f32[3,8,1,128]{3,1,2,0:T(8,128)S(1)}, f32[3,8,1,128]{3,1,2,0:T(8,128)S(1)}, u32[]{:S(2)}, u32[]{:S(2)}) collective-permute-start(f32[3,8,1,128]{3,1,2,0:T(8,128)S(1)} %bitcast.305), channel_id=1, source_target_pairs={{0,4},{4,8},{8,12},{12,16},{16,20},{20,24},{24,28},{1,5},{5,9},{9,... | collective-permute-start | bytes 36872 | tf_op jit(solution)/shard_map/ppermute | solution.py:31
  107.4 16.5 %collective-permute-start.19 = (f32[3,1,16,128]{3,2,1,0:T(8,128)S(1)}, f32[3,1,16,128]{3,2,1,0:T(8,128)S(1)}, u32[]{:S(2)}, u32[]{:S(2)}) collective-permute-start(f32[3,1,16,128]{3,2,1,0:T(8,128)S(1)} %get-tuple-element.169), channel_id=1, source_target_pairs={{0,32},{32,64},{64,96},{96,128},{128,160},{160,192},{192,224},{1,3... | collective-permute-start | bytes 73736 | tf_op jit(solution)/shard_map/ppermute | solution.py:31
  189.9 17.4 %collective-permute-start.45 = (f32[3,8,1,128]{3,1,2,0:T(8,128)S(1)}, f32[3,8,1,128]{3,1,2,0:T(8,128)S(1)}, u32[]{:S(2)}, u32[]{:S(2)}) collective-permute-start(f32[3,8,1,128]{3,1,2,0:T(8,128)S(1)} %bitcast.306), channel_id=1, source_target_pairs={{0,4},{4,8},{8,12},{12,16},{16,20},{20,24},{24,28},{1,5},{5,9},{9,... | collective-permute-start | bytes 36872 | tf_op jit(solution)/shard_map/ppermute | solution.py:31
  212.4 17.7 %collective-permute-start.51 = (f32[3,8,1,128]{3,1,2,0:T(8,128)S(1)}, f32[3,8,1,128]{3,1,2,0:T(8,128)S(1)}, u32[]{:S(2)}, u32[]{:S(2)}) collective-permute-start(f32[3,8,1,128]{3,1,2,0:T(8,128)S(1)} %bitcast.307), channel_id=1, source_target_pairs={{0,4},{4,8},{8,12},{12,16},{16,20},{20,24},{24,28},{1,5},{5,9},{9,... | collective-permute-start | bytes 36872 | tf_op jit(solution)/shard_map/ppermute | solution.py:31
  281.3 26.9 %collective-permute-start.56 = (f32[4,8,1,128]{3,1,2,0:T(8,128)S(1)}, f32[4,8,1,128]{3,1,2,0:T(8,128)S(1)}, u32[]{:S(2)}, u32[]{:S(2)}) collective-permute-start(f32[4,8,1,128]{3,1,2,0:T(8,128)S(1)} %bitcast.272), channel_id=1, source_target_pairs={{4,0},{8,4},{12,8},{16,12},{20,16},{24,20},{28,24},{5,1},{9,5},{13... | collective-permute-start | bytes 49160 | tf_op jit(solution)/shard_map/ppermute | solution.py:32
  285.6 22.7 %collective-permute-start.57 = (f32[4,8,1,128]{3,1,2,0:T(8,128)S(1)}, f32[4,8,1,128]{3,1,2,0:T(8,128)S(1)}, u32[]{:S(2)}, u32[]{:S(2)}) collective-permute-start(f32[4,8,1,128]{3,1,2,0:T(8,128)S(1)} %bitcast.269), channel_id=1, source_target_pairs={{0,4},{4,8},{8,12},{12,16},{16,20},{20,24},{24,28},{1,5},{5,9},{9,... | collective-permute-start | bytes 49160 | tf_op jit(solution)/shard_map/ppermute | solution.py:31
  287.5 20.8 %collective-permute-start.55 = (f32[4,1,16,128]{3,2,1,0:T(8,128)S(1)}, f32[4,1,16,128]{3,2,1,0:T(8,128)S(1)}, u32[]{:S(2)}, u32[]{:S(2)}) collective-permute-start(f32[4,1,16,128]{3,2,1,0:T(8,128)S(1)} %get-tuple-element.86), channel_id=1, source_target_pairs={{0,32},{32,64},{64,96},{96,128},{128,160},{160,192},{192,224},{1,3... | collective-permute-start | bytes 98312 | tf_op jit(solution)/shard_map/ppermute | solution.py:31
  290.8 17.5 %collective-permute-start.54 = (f32[4,1,16,128]{3,2,1,0:T(8,128)S(1)}, f32[4,1,16,128]{3,2,1,0:T(8,128)S(1)}, u32[]{:S(2)}, u32[]{:S(2)}) collective-permute-start(f32[4,1,16,128]{3,2,1,0:T(8,128)S(1)} %get-tuple-element.87), channel_id=1, source_target_pairs={{32,0},{64,32},{96,64},{128,96},{160,128},{192,160},{224,192},{33,... | collective-permute-start | bytes 98312 | tf_op jit(solution)/shard_map/ppermute | solution.py:32
  393.2 16.6 %collective-permute-start.81 = (f32[3,8,1,128]{3,1,2,0:T(8,128)S(1)}, f32[3,8,1,128]{3,1,2,0:T(8,128)S(1)}, u32[]{:S(2)}, u32[]{:S(2)}) collective-permute-start(f32[3,8,1,128]{3,1,2,0:T(8,128)S(1)} %bitcast.309), channel_id=1, source_target_pairs={{0,4},{4,8},{8,12},{12,16},{16,20},{20,24},{24,28},{1,5},{5,9},{9,... | collective-permute-start | bytes 36872 | tf_op jit(solution)/shard_map/ppermute | solution.py:31
  416.2 16.9 %collective-permute-start.87 = (f32[3,8,1,128]{3,1,2,0:T(8,128)S(1)}, f32[3,8,1,128]{3,1,2,0:T(8,128)S(1)}, u32[]{:S(2)}, u32[]{:S(2)}) collective-permute-start(f32[3,8,1,128]{3,1,2,0:T(8,128)S(1)} %bitcast.310), channel_id=1, source_target_pairs={{0,4},{4,8},{8,12},{12,16},{16,20},{20,24},{24,28},{1,5},{5,9},{9,... | collective-permute-start | bytes 36872 | tf_op jit(solution)/shard_map/ppermute | solution.py:31
  420.5 16.0 %collective-permute-start.85 = (f32[3,1,16,128]{3,2,1,0:T(8,128)S(1)}, f32[3,1,16,128]{3,2,1,0:T(8,128)S(1)}, u32[]{:S(2)}, u32[]{:S(2)}) collective-permute-start(f32[3,1,16,128]{3,2,1,0:T(8,128)S(1)} %get-tuple-element.141), channel_id=1, source_target_pairs={{0,32},{32,64},{64,96},{96,128},{128,160},{160,192},{192,224},{1,3... | collective-permute-start | bytes 73736 | tf_op jit(solution)/shard_map/ppermute | solution.py:31
  484.0 26.9 %collective-permute-start.92 = (f32[4,8,1,128]{3,1,2,0:T(8,128)S(1)}, f32[4,8,1,128]{3,1,2,0:T(8,128)S(1)}, u32[]{:S(2)}, u32[]{:S(2)}) collective-permute-start(f32[4,8,1,128]{3,1,2,0:T(8,128)S(1)} %bitcast.273), channel_id=1, source_target_pairs={{4,0},{8,4},{12,8},{16,12},{20,16},{24,20},{28,24},{5,1},{9,5},{13... | collective-permute-start | bytes 49160 | tf_op jit(solution)/shard_map/ppermute | solution.py:32
  488.3 22.7 %collective-permute-start.93 = (f32[4,8,1,128]{3,1,2,0:T(8,128)S(1)}, f32[4,8,1,128]{3,1,2,0:T(8,128)S(1)}, u32[]{:S(2)}, u32[]{:S(2)}) collective-permute-start(f32[4,8,1,128]{3,1,2,0:T(8,128)S(1)} %bitcast.270), channel_id=1, source_target_pairs={{0,4},{4,8},{8,12},{12,16},{16,20},{20,24},{24,28},{1,5},{5,9},{9,... | collective-permute-start | bytes 49160 | tf_op jit(solution)/shard_map/ppermute | solution.py:31
  490.2 20.8 %collective-permute-start.91 = (f32[4,1,16,128]{3,2,1,0:T(8,128)S(1)}, f32[4,1,16,128]{3,2,1,0:T(8,128)S(1)}, u32[]{:S(2)}, u32[]{:S(2)}) collective-permute-start(f32[4,1,16,128]{3,2,1,0:T(8,128)S(1)} %get-tuple-element.80), channel_id=1, source_target_pairs={{0,32},{32,64},{64,96},{96,128},{128,160},{160,192},{192,224},{1,3... | collective-permute-start | bytes 98312 | tf_op jit(solution)/shard_map/ppermute | solution.py:31
  493.6 17.4 %collective-permute-start.90 = (f32[4,1,16,128]{3,2,1,0:T(8,128)S(1)}, f32[4,1,16,128]{3,2,1,0:T(8,128)S(1)}, u32[]{:S(2)}, u32[]{:S(2)}) collective-permute-start(f32[4,1,16,128]{3,2,1,0:T(8,128)S(1)} %get-tuple-element.81), channel_id=1, source_target_pairs={{32,0},{64,32},{96,64},{128,96},{160,128},{192,160},{224,192},{33,... | collective-permute-start | bytes 98312 | tf_op jit(solution)/shard_map/ppermute | solution.py:32
  594.8 16.8 %collective-permute-start.117 = (f32[3,8,1,128]{3,1,2,0:T(8,128)S(1)}, f32[3,8,1,128]{3,1,2,0:T(8,128)S(1)}, u32[]{:S(2)}, u32[]{:S(2)}) collective-permute-start(f32[3,8,1,128]{3,1,2,0:T(8,128)S(1)} %bitcast.312), channel_id=1, source_target_pairs={{0,4},{4,8},{8,12},{12,16},{16,20},{20,24},{24,28},{1,5},{5,9},{9,... | collective-permute-start | bytes 36872 | tf_op jit(solution)/shard_map/ppermute | solution.py:31
  616.7 16.9 %collective-permute-start.123 = (f32[3,8,1,128]{3,1,2,0:T(8,128)S(1)}, f32[3,8,1,128]{3,1,2,0:T(8,128)S(1)}, u32[]{:S(2)}, u32[]{:S(2)}) collective-permute-start(f32[3,8,1,128]{3,1,2,0:T(8,128)S(1)} %bitcast.313), channel_id=1, source_target_pairs={{0,4},{4,8},{8,12},{12,16},{16,20},{20,24},{24,28},{1,5},{5,9},{9,... | collective-permute-start | bytes 36872 | tf_op jit(solution)/shard_map/ppermute | solution.py:31
  620.9 16.0 %collective-permute-start.121 = (f32[3,1,16,128]{3,2,1,0:T(8,128)S(1)}, f32[3,1,16,128]{3,2,1,0:T(8,128)S(1)}, u32[]{:S(2)}, u32[]{:S(2)}) collective-permute-start(f32[3,1,16,128]{3,2,1,0:T(8,128)S(1)} %get-tuple-element.123), channel_id=1, source_target_pairs={{0,32},{32,64},{64,96},{96,128},{128,160},{160,192},{192,224},{1,3... | collective-permute-start | bytes 73736 | tf_op jit(solution)/shard_map/ppermute | solution.py:31
  684.3 26.9 %collective-permute-start.128 = (f32[4,8,1,128]{3,1,2,0:T(8,128)S(1)}, f32[4,8,1,128]{3,1,2,0:T(8,128)S(1)}, u32[]{:S(2)}, u32[]{:S(2)}) collective-permute-start(f32[4,8,1,128]{3,1,2,0:T(8,128)S(1)} %bitcast.274), channel_id=1, source_target_pairs={{4,0},{8,4},{12,8},{16,12},{20,16},{24,20},{28,24},{5,1},{9,5},{13... | collective-permute-start | bytes 49160 | tf_op jit(solution)/shard_map/ppermute | solution.py:32
  688.6 22.7 %collective-permute-start.129 = (f32[4,8,1,128]{3,1,2,0:T(8,128)S(1)}, f32[4,8,1,128]{3,1,2,0:T(8,128)S(1)}, u32[]{:S(2)}, u32[]{:S(2)}) collective-permute-start(f32[4,8,1,128]{3,1,2,0:T(8,128)S(1)} %bitcast.271), channel_id=1, source_target_pairs={{0,4},{4,8},{8,12},{12,16},{16,20},{20,24},{24,28},{1,5},{5,9},{9,... | collective-permute-start | bytes 49160 | tf_op jit(solution)/shard_map/ppermute | solution.py:31
  690.5 20.8 %collective-permute-start.127 = (f32[4,1,16,128]{3,2,1,0:T(8,128)S(1)}, f32[4,1,16,128]{3,2,1,0:T(8,128)S(1)}, u32[]{:S(2)}, u32[]{:S(2)}) collective-permute-start(f32[4,1,16,128]{3,2,1,0:T(8,128)S(1)} %get-tuple-element.74), channel_id=1, source_target_pairs={{0,32},{32,64},{64,96},{96,128},{128,160},{160,192},{192,224},{1,3... | collective-permute-start | bytes 98312 | tf_op jit(solution)/shard_map/ppermute | solution.py:31
  693.9 17.4 %collective-permute-start.126 = (f32[4,1,16,128]{3,2,1,0:T(8,128)S(1)}, f32[4,1,16,128]{3,2,1,0:T(8,128)S(1)}, u32[]{:S(2)}, u32[]{:S(2)}) collective-permute-start(f32[4,1,16,128]{3,2,1,0:T(8,128)S(1)} %get-tuple-element.75), channel_id=1, source_target_pairs={{32,0},{64,32},{96,64},{128,96},{160,128},{192,160},{224,192},{33,... | collective-permute-start | bytes 98312 | tf_op jit(solution)/shard_map/ppermute | solution.py:32
  793.1 17.0 %collective-permute-start.153 = (f32[3,8,1,128]{3,1,2,0:T(8,128)S(1)}, f32[3,8,1,128]{3,1,2,0:T(8,128)S(1)}, u32[]{:S(2)}, u32[]{:S(2)}) collective-permute-start(f32[3,8,1,128]{3,1,2,0:T(8,128)S(1)} %bitcast.315), channel_id=1, source_target_pairs={{0,4},{4,8},{8,12},{12,16},{16,20},{20,24},{24,28},{1,5},{5,9},{9,... | collective-permute-start | bytes 36872 | tf_op jit(solution)/shard_map/ppermute | solution.py:31
  815.2 16.9 %collective-permute-start.159 = (f32[3,8,1,128]{3,1,2,0:T(8,128)S(1)}, f32[3,8,1,128]{3,1,2,0:T(8,128)S(1)}, u32[]{:S(2)}, u32[]{:S(2)}) collective-permute-start(f32[3,8,1,128]{3,1,2,0:T(8,128)S(1)} %bitcast.316), channel_id=1, source_target_pairs={{0,4},{4,8},{8,12},{12,16},{16,20},{20,24},{24,28},{1,5},{5,9},{9,... | collective-permute-start | bytes 36872 | tf_op jit(solution)/shard_map/ppermute | solution.py:31
  (173 other events, 3209.4 us)
where the time goes:
time: 899 us; the launch traced here: 885 us
  starting transfers between devices  468 us (52%)
  blocking collectives  185 us (21%)
  waiting for transfers between devices  95.9 us (11%)
  local copies, waits for them, and re-layouts  81 us (9%)
  other arithmetic  47.3 us (5%)
    ppermute x81, starting transfers between devices, extended(): lax.ppermute(last, axis, up)  334 us
    psum x16, blocking collectives, by_axis(): value = lax.psum(value, axis)  185 us
    ppermute x81, starting transfers between devices, extended(): lax.ppermute(initial, axis, [(b, a) for a, b in up])  134 us
    reshape x5, local copies, waits for them, and re-layouts, restrict(): field.reshape(leading + (cells_x // 2, 2, cells_y // 2, 2, cells_z // 2, 2))  61.2 us
    ppermute x81, waiting for transfers between devices, extended(): lax.ppermute(initial, axis, [(b, a) for a, b in up])  53.9 us
    ppermute x81, waiting for transfers between devices, extended(): lax.ppermute(last, axis, up)  41.9 us
    reduce_sum x5, other arithmetic, restrict(): return blocks.mean(axis=(-5, -3, -1))  24.6 us
  transfers between devices with their start and end apart: 162, of which 41 were waited for; matrix products, arithmetic and copies ran while one was open for 1% of the time, Pallas kernels for 0%

commit v1 on v0

v1 whole, which is shorter than its diff:
```python
import functools

import jax
import jax.numpy as jnp
from jax import lax
from jax.experimental import pallas as pl
from jax.experimental.pallas import tpu as pltpu
from jax.sharding import PartitionSpec as P

RECOMPUTE = 2
SCHUR_ITERS = 4
COARSE_SWEEPS = 3
LAYERS = 8
INCREMENT_DT = 0.2
DIFFUSIVITY = 0.3
ACTIVATION_ENERGY = 2.3
JACOBI_WEIGHT = 0.7
SCHUR_WEIGHT = 0.5
RAYLEIGH = 1.0

MESH = pl.DeviceIdType.MESH
AXES = ("gx", "gy", "gz")
NX, NY, NZ = 8, 16, 128
CX = NX // 2
PITCH = 24
FIRST = 8
KEEP = 1.0 - JACOBI_WEIGHT

HEAT1, HEAT2, FIELDS, PRESSURE, FIRST_SMOOTH, SWEEP1, SWEEP2, LAST_SMOOTH, VELOCITY = range(9)
ROUNDS = 9


def row(plane):
    return FIRST + plane * PITCH


class Item:
    def __init__(self, ref, comps, planes, width, xoff=0, yoff=0, lane=0, first=0):
        self.ref, self.comps, self.planes, self.width = ref, comps, planes, width
        self.xoff, self.yoff, self.lane, self.first = xoff, yoff, lane, first

    def count(self):
        return self.comps * self.planes

    def spot(self, c, x):
        return self.lane + (c * self.planes + x) * 2 * self.width


def kernel(sizes, total_cells, heat, motion, dual, rheology, stiffness, out_t, out_v, out_p, fine, coarse, vel, press,
           fields, cvisc, res, src, adj, held, cres, trans, kf, kc, kh, aux, xs, xr, ys, yr, zs, zr, psum, mean, ar_out,
           ar_in, send_sem, recv_sem, ar_send, ar_recv):
    at = [lax.axis_index(a) for a in AXES]
    barrier = pltpu.get_barrier_semaphore()
    peers = sum(n - 1 for n in sizes)
    for axis, me, n in zip(AXES, at, sizes):
        for d in range(1, n):
            pl.semaphore_signal(barrier, inc=1, device_id={axis: lax.rem(me + d, n)}, device_id_type=MESH)

    lanes = lax.broadcasted_iota(jnp.int32, (NY, NZ), 1)
    rows = lax.broadcasted_iota(jnp.int32, (NY, NZ), 0)
    pair = {1: lanes >> 1, 2: lanes >> 2}
    upper = {1: (lanes & 1) == 1, 2: (lanes & 3) >= 2}
    low = {1: lanes < 1, 2: lanes < 2}
    high = {1: lanes >= NZ - 1, 2: lanes >= NZ - 2}
    even_row = (rows & 1) == 0
    even_lane = (lanes & 1) == 0

    def lroll(v, shift):
        return pltpu.roll(v, shift % NZ, 1)

    def copies(t, xrows, yrows):
        out = []
        for k, (axis, me, n) in enumerate(zip(AXES, at, sizes)):
            for s in (0, 1):
                source = (xs.at[t, s, pl.ds(0, xrows)], ys.at[t, s, pl.ds(0, yrows)], zs.at[t])[k]
                target = (xr.at[t, s, pl.ds(0, xrows)], yr.at[t, s, pl.ds(0, yrows)], zr.at[t, s])[k]
                peer = lax.rem(me + (1 if s == 0 else n - 1), n)
                copy = pltpu.make_async_remote_copy(
                    src_ref=source, dst_ref=target, send_sem=send_sem.at[t, 2 * k + s],
                    recv_sem=recv_sem.at[t, 2 * k + s], device_id={axis: peer}, device_id_type=MESH)
                up, down = me < n - 1, me > 0
                out.append((copy, up if s == 0 else down, down if s == 0 else up))
        return out

    def start(t, xrows, yrows):
        for copy, sends, _ in copies(t, xrows, yrows):
            pl.when(sends)(copy.start)

    def finish(t, xrows, yrows):
        for copy, _, gets in copies(t, xrows, yrows):
            pl.when(gets)(copy.wait_recv)
        for copy, sends, _ in copies(t, xrows, yrows):
            pl.when(sends)(copy.wait_send)

    def pack_lanes(acc, value, spot, w):
        return jnp.where(pair[w] == spot // (2 * w), lroll(value, spot + w), acc)

    def chunks(n):
        return [(a, min(8, n - a)) for a in range(0, n, 8)]

    def pack(t, items):
        acc = jnp.zeros((NY, NZ), jnp.float32)
        for it in items:
            for c in range(it.comps):
                p = (it.first + c) * it.planes
                at_row = it.xoff + c * NY
                xs[t, 0, at_row:at_row + NY] = it.ref[row(p + it.planes - 1):row(p + it.planes - 1) + NY]
                xs[t, 1, at_row:at_row + NY] = it.ref[row(p):row(p) + NY]
            base = row(it.first * it.planes)
            for a, size in chunks(it.count()):
                ys[t, 0, it.yoff + a:it.yoff + a + size] = it.ref[pl.ds(base + a * PITCH + NY - 1, size, stride=PITCH), :]
                ys[t, 1, it.yoff + a:it.yoff + a + size] = it.ref[pl.ds(base + a * PITCH, size, stride=PITCH), :]
            for c in range(it.comps):
                for x in range(it.planes):
                    r = row((it.first + c) * it.planes + x)
                    acc = pack_lanes(acc, it.ref[r:r + NY], it.spot(c, x), it.width)
        zs[t] = acc

    def unpack(t, it, low_extra=None, high_extra=None):
        base = row(it.first * it.planes)
        for a, size in chunks(it.count()):
            below, above = yr[t, 0, it.yoff + a:it.yoff + a + size], yr[t, 1, it.yoff + a:it.yoff + a + size]
            if low_extra is not None:
                below, above = below + low_extra[:size], above + high_extra[:size]
            for k in range(it.width):
                it.ref[pl.ds(base + a * PITCH - 1 - k, size, stride=PITCH), :] = below
                it.ref[pl.ds(base + a * PITCH + NY + k, size, stride=PITCH), :] = above
        return jnp.where(upper[it.width], lroll(zr[t, 0], it.width), lroll(zr[t, 1], -it.width))

    def sides(t, it, c, x):
        r, k = row((it.first + c) * it.planes + x), it.xoff + c * NY
        here = it.ref[r:r + NY]
        xm = xr[t, 0, k:k + NY] if x == 0 else it.ref[r - PITCH:r - PITCH + NY]
        xp = xr[t, 1, k:k + NY] if x == it.planes - 1 else it.ref[r + PITCH:r + PITCH + NY]
        w = it.width
        return here, xm, xp, it.ref[r - w:r - w + NY], it.ref[r + w:r + w + NY]

    def edge(it, c, x, zpairs):
        return lroll(zpairs, -(it.spot(c, x) + it.width))

    def ends(here, at_edge, w):
        return jnp.where(low[w], at_edge, lroll(here, w)), jnp.where(high[w], at_edge, lroll(here, -w))

    def coefs(k, x):
        return [k[n, x * NY:(x + 1) * NY] for n in range(7)]

    def set_coefs(k, x, six, w):
        xm, xp, ym, yp, zm, zp = six
        for n, v in enumerate((xm, xp, ym, yp, jnp.where(low[w], 0.0, zm), jnp.where(high[w], 0.0, zp),
                               jnp.where(low[w], zm, jnp.where(high[w], zp, 0.0)))):
            k[n, x * NY:(x + 1) * NY] = v

    def gather(t, it, c, x, k, zpairs):
        here, xm, xp, ym, yp = sides(t, it, c, x)
        w = it.width
        total = (k[0] * xm + k[1] * xp) + (k[2] * ym + k[3] * yp)
        total = total + (k[4] * lroll(here, w) + k[5] * lroll(here, -w)) + k[6] * edge(it, c, x, zpairs)
        return total, here

    def put(ref, plane, value):
        ref[row(plane):row(plane) + NY] = value

    def get(ref, plane):
        return ref[row(plane):row(plane) + NY]

    def flat(plane):
        return slice(plane * NY, (plane + 1) * NY)

    def restrict_pair(a, b):
        s = a + b
        s = s + jnp.where(even_row, pltpu.roll(s, NY - 1, 0), pltpu.roll(s, 1, 0))
        s = s + jnp.where(even_lane, lroll(s, -1), lroll(s, 1))
        return 0.125 * s

    order = (1, 2, 0)
    base_slot = {}
    slots = 0
    for axis in order:
        base_slot[axis] = slots
        slots += sizes[axis] - 1

    def ar_copies(axis, turn):
        n, me = sizes[axis], at[axis]
        out = []
        for d in range(1, n):
            slot = base_slot[axis] + d - 1
            out.append(pltpu.make_async_remote_copy(
                src_ref=ar_out.at[turn, order.index(axis)], dst_ref=ar_in.at[turn, slot],
                send_sem=ar_send.at[turn, slot], recv_sem=ar_recv.at[turn, slot],
                device_id={AXES[axis]: lax.rem(me + d, n)}, device_id_type=MESH))
        return out

    def ar_start(stage, turn):
        ar_out[turn, stage] = psum[...]
        for copy in ar_copies(order[stage], turn):
            copy.start()

    def ar_finish(stage, turn):
        axis = order[stage]
        pending = ar_copies(axis, turn)
        total = psum[...]
        for copy in pending:
            copy.wait_recv()
        for d in range(1, sizes[axis]):
            total = total + ar_in[turn, base_slot[axis] + d - 1]
        psum[...] = total
        for copy in pending:
            copy.wait_send()

    def put_sum(value):
        s = jnp.sum(jnp.sum(value, axis=0, keepdims=True), axis=1, keepdims=True)
        psum[...] = jnp.broadcast_to(s, (8, NZ))

    def add_mean():
        mean[0] = mean[0] + psum[...]
        mean[1] = mean[1] + (0.5 / total_cells) * mean[0]

    for k, (me, n) in enumerate(zip(at, sizes)):
        for s, gone in ((0, me == 0), (1, me == n - 1)):
            @pl.when(gone)
            def _():
                for t in range(ROUNDS):
                    into = (xr, yr, zr)[k]
                    into[t, s] = jnp.zeros(into.shape[2:], jnp.float32)

    mean[...] = jnp.zeros_like(mean)
    heat_item = Item(fields, 1, NX, 1)
    trans_item = Item(trans, 1, NX, 1, xoff=NY, yoff=NX, lane=2 * NX)
    spread, step = INCREMENT_DT * DIFFUSIVITY, INCREMENT_DT
    for x in range(NX):
        put(fields, x, heat[x])
        lam = dual[x]
        six, total = [], 0.0
        for k in range(3):
            m = motion[k, x]
            am, ap = spread + step * jnp.maximum(m, 0.0), spread - step * jnp.minimum(m, 0.0)
            six += [am, ap]
            total = total + am + ap
        set_coefs(kh, x, six, 1)
        aux[0, flat(x)] = 1.0 - total
        if x == 0:
            xs[HEAT1, 1, NY:2 * NY] = six[0] * lam
        if x == NX - 1:
            xs[HEAT1, 0, NY:2 * NY] = six[1] * lam
        put(trans, x, six[3] * lam)
        put(trans, NX + x, six[2] * lam)
    acc = jnp.zeros((NY, NZ), jnp.float32)
    xs[HEAT1, 0, 0:NY] = heat[NX - 1]
    xs[HEAT1, 1, 0:NY] = heat[0]
    ys[HEAT1, 0, 0:NX] = fields[pl.ds(FIRST + NY - 1, NX, stride=PITCH), :]
    ys[HEAT1, 1, 0:NX] = fields[pl.ds(FIRST, NX, stride=PITCH), :]
    ys[HEAT1, 0, NX:2 * NX] = trans[pl.ds(FIRST + NY - 1, NX, stride=PITCH), :]
    ys[HEAT1, 1, NX:2 * NX] = trans[pl.ds(row(NX), NX, stride=PITCH), :]
    for x in range(NX):
        lam = dual[x]
        acc = pack_lanes(acc, heat[x], heat_item.spot(0, x), 1)
        am = spread + step * jnp.maximum(motion[2, x], 0.0)
        ap = spread - step * jnp.minimum(motion[2, x], 0.0)
        acc = pack_lanes(acc, jnp.where(low[1], am * lam, ap * lam), trans_item.spot(0, x), 1)
    zs[HEAT1] = acc
    pl.semaphore_wait(barrier, peers)
    start(HEAT1, 2 * NY, 2 * NX)
    for x in range(NX):
        base = jnp.zeros((NY, NZ), jnp.float32)
        for layer in range(LAYERS):
            base = jnp.where(rheology[x] == layer, stiffness[layer], base)
        aux[1, flat(x)] = base
    finish(HEAT1, 2 * NY, 2 * NX)

    zpairs = unpack(HEAT1, heat_item)
    stepped = []
    for x in range(NX):
        total, here = gather(HEAT1, heat_item, 0, x, coefs(kh, x), zpairs)
        stepped.append(aux[0, flat(x)] * here + total)
    for x in range(NX):
        put(fields, x, stepped[x])
    pack(HEAT2, [heat_item])
    start(HEAT2, NY, NX)

    for a in (0,):
        trans[pl.ds(row(0) - 1, NX, stride=PITCH), :] = yr[HEAT1, 0, NX:2 * NX]
        trans[pl.ds(row(NX) + NY, NX, stride=PITCH), :] = yr[HEAT1, 1, NX:2 * NX]
    for x in range(NX):
        lam = dual[x]
        ap_x = lambda i: (spread - step * jnp.minimum(motion[0, i], 0.0)) * dual[i]
        am_x = lambda i: (spread + step * jnp.maximum(motion[0, i], 0.0)) * dual[i]
        below = xr[HEAT1, 0, NY:2 * NY] if x == 0 else ap_x(x - 1)
        above = xr[HEAT1, 1, NY:2 * NY] if x == NX - 1 else am_x(x + 1)
        r = row(x)
        total = aux[0, flat(x)] * lam + below + above
        total = total + trans[r - 1:r - 1 + NY] + trans[row(NX + x) + 1:row(NX + x) + 1 + NY]
        am = spread + step * jnp.maximum(motion[2, x], 0.0)
        ap = spread - step * jnp.minimum(motion[2, x], 0.0)
        at_edge = edge(trans_item, 0, x, zpairs)
        total = total + jnp.where(low[1], at_edge, lroll(ap * lam, 1)) + jnp.where(high[1], at_edge, lroll(am * lam, -1))
        out_t[x] = total
    finish(HEAT2, NY, NX)

    zpairs = unpack(HEAT2, heat_item)
    stepped = []
    for x in range(NX):
        total, here = gather(HEAT2, heat_item, 0, x, coefs(kh, x), zpairs)
        stepped.append(aux[0, flat(x)] * here + total)
    for x in range(NX):
        put(fields, x, stepped[x])
        put(fields, NX + x, aux[1, flat(x)] * jnp.exp(-ACTIVATION_ENERGY * stepped[x]))
    for x in range(CX):
        put(cvisc, x, restrict_pair(get(fields, NX + 2 * x), get(fields, NX + 2 * x + 1)))
    both = Item(fields, 2, NX, 1)
    cv_item = Item(cvisc, 1, CX, 2, xoff=2 * NY, yoff=2 * NX, lane=64)
    pack(FIELDS, [both, cv_item])
    start(FIELDS, 3 * NY, 2 * NX + 8)
    finish(FIELDS, 3 * NY, 2 * NX + 8)

    zpairs = unpack(FIELDS, both)
    cpairs = unpack(FIELDS, cv_item)
    for x in range(NX):
        here, xm, xp, ym, yp = sides(FIELDS, both, 0, x)
        zm, zp = ends(here, edge(both, 0, x, zpairs), 1)
        lam = -INCREMENT_DT * dual[x]
        for k, (m, p) in enumerate(((xm, xp), (ym, yp), (zm, zp))):
            src[flat(k * NX + x)] = lam * jnp.where(motion[k, x] > 0, here - m, p - here)
        here, xm, xp, ym, yp = sides(FIELDS, both, 1, x)
        zm, zp = ends(here, edge(both, 1, x, zpairs), 1)
        six = [0.5 * (here + v) for v in (xm, xp, ym, yp, zm, zp)]
        set_coefs(kf, x, six, 1)
        diagonal = (six[0] + six[1]) + (six[2] + six[3]) + (six[4] + six[5])
        inverse = JACOBI_WEIGHT / diagonal
        aux[2, flat(x)] = diagonal
        aux[3, flat(x)] = inverse
        aux[4, flat(x)] = (0.5 * SCHUR_WEIGHT) * here
        for k, (m, p) in enumerate(((xm, xp), (ym, yp), (zm, zp))):
            g = 0.5 * (p - m)
            s = src[flat(k * NX + x)]
            res[flat((3 + k) * NX + x)] = g
            res[flat(k * NX + x)] = s
            put(fine, (3 + k) * NX + x, inverse * g)
            put(fine, k * NX + x, inverse * s)
    for x in range(CX):
        here, xm, xp, ym, yp = sides(FIELDS, cv_item, 0, x)
        zm, zp = ends(here, edge(cv_item, 0, x, cpairs), 2)
        six = [0.125 * (here + v) for v in (xm, xp, ym, yp, zm, zp)]
        set_coefs(kc, x, six, 2)
        aux[5, flat(x)] = JACOBI_WEIGHT / ((six[0] + six[1]) + (six[2] + six[3]) + (six[4] + six[5]))

    def cycle(nc, during, first):
        fi, ci = Item(fine, nc, NX, 1), Item(coarse, nc, CX, 2)
        fx, fy, cx, cy = nc * NY, nc * NX, nc * NY, (nc * CX + 7) // 8 * 8
        pack(FIRST_SMOOTH, [fi])
        start(FIRST_SMOOTH, fx, fy)
        during(0)
        finish(FIRST_SMOOTH, fx, fy)
        zpairs = unpack(FIRST_SMOOTH, fi)
        for x in range(CX):
            inv_c = aux[5, flat(x)]
            ka, kb = coefs(kf, 2 * x), coefs(kf, 2 * x + 1)
            for c in range(nc):
                pa, pb = c * NX + 2 * x, c * NX + 2 * x + 1
                a = KEEP * res[flat(pa)] + gather(FIRST_SMOOTH, fi, c, 2 * x, ka, zpairs)[0]
                b = KEEP * res[flat(pb)] + gather(FIRST_SMOOTH, fi, c, 2 * x + 1, kb, zpairs)[0]
                if first and c >= 3:
                    held[flat(pa - 3 * NX)] = a
                    held[flat(pb - 3 * NX)] = b
                r = restrict_pair(a, b)
                cres[flat(c * CX + x)] = r
                put(coarse, c * CX + x, inv_c * r)
        for sweep in range(COARSE_SWEEPS - 1):
            t = SWEEP1 + sweep
            pack(t, [ci])
            start(t, cx, cy)
            during(1 + sweep)
            finish(t, cx, cy)
            cpairs = unpack(t, ci)
            last = sweep == COARSE_SWEEPS - 2
            swept = []
            for x in range(CX):
                inv_c = aux[5, flat(x)]
                k = coefs(kc, x)
                for c in range(nc):
                    total, here = gather(t, ci, c, x, k, cpairs)
                    e = KEEP * here + inv_c * (cres[flat(c * CX + x)] + total)
                    if last:
                        for q in (2 * x, 2 * x + 1):
                            put(fine, c * NX + q, get(fine, c * NX + q) + e)
                    else:
                        swept.append((c * CX + x, e))
            for plane, e in swept:
                put(coarse, plane, e)
        pack(LAST_SMOOTH, [fi])
        start(LAST_SMOOTH, fx, fy)
        during(3)
        finish(LAST_SMOOTH, fx, fy)
        zpairs = unpack(LAST_SMOOTH, fi)
        for x in range(NX):
            k = coefs(kf, x)
            inverse = aux[3, flat(x)]
            for c in range(nc):
                total, here = gather(LAST_SMOOTH, fi, c, x, k, zpairs)
                new = KEEP * here + inverse * (res[flat(c * NX + x)] + total)
                if c >= 3:
                    adj[flat((c - 3) * NX + x)] = new
                elif first:
                    put(vel, c * NX + x, new)
                else:
                    put(vel, c * NX + x, get(vel, c * NX + x) + new)

    vel_item, press_item = Item(vel, 3, NX, 1), Item(press, 1, NX, 1)

    def divergence(during, first):
        pack(VELOCITY, [vel_item])
        start(VELOCITY, 3 * NY, 3 * NX)
        during()
        finish(VELOCITY, 3 * NY, 3 * NX)
        zpairs = unpack(VELOCITY, vel_item)
        for x in range(NX):
            _, xm, xp, _, _ = sides(VELOCITY, vel_item, 0, x)
            _, _, _, ym, yp = sides(VELOCITY, vel_item, 1, x)
            here = get(vel, 2 * NX + x)
            zm, zp = ends(here, edge(vel_item, 2, x, zpairs), 1)
            change = aux[4, flat(x)] * ((xp - xm) + (yp - ym) + (zp - zm))
            put(press, x, -change if first else get(press, x) - change)

    def first_during(stage):
        if stage == 3:
            acc = jnp.zeros((NY, NZ), jnp.float32)
            for x in range(NX):
                inverse = aux[3, flat(x)]
                for c in range(3):
                    p = c * NX + x
                    acc = acc + held[flat(p)] * get(fine, p)
                    acc = acc + (inverse * res[flat(3 * NX + p)]) * res[flat(p)]
            put_sum(acc)
            ar_start(0, 0)

    cycle(6, first_during, True)

    def first_sum():
        ar_finish(0, 0)
        ar_start(1, 0)

    divergence(first_sum, True)
    ar_finish(1, 0)
    ar_start(2, 0)

    lowest = [jnp.where(me == 0, 1.0, 0.0) for me in at]
    highest = [jnp.where(me == n - 1, 1.0, 0.0) for me, n in zip(at, sizes)]

    def iteration(turn, carry):
        pack(PRESSURE, [press_item])
        start(PRESSURE, NY, NX)
        zpairs = jnp.where(upper[1], lroll(zr[VELOCITY, 0], 1), lroll(zr[VELOCITY, 1], -1))
        for x in range(NX):
            k = coefs(kf, x)
            diagonal = aux[2, flat(x)]
            for c in range(3):
                total, here = gather(VELOCITY, vel_item, c, x, k, zpairs)
                res[flat(c * NX + x)] = src[flat(c * NX + x)] - diagonal * here + total
        finish(PRESSURE, NY, NX)
        ar_finish(2, turn - 1)
        add_mean()
        m8 = mean[1]
        m = jnp.concatenate([m8, m8], axis=0)
        zpairs = unpack(PRESSURE, press_item, lowest[1] * m8, highest[1] * m8)
        zfill = jnp.where(low[1], lowest[2], highest[2]) * m
        for x in range(NX):
            inverse = aux[3, flat(x)]
            here, xm, xp, ym, yp = sides(PRESSURE, press_item, 0, x)
            if x == 0:
                xm = xm + lowest[0] * m
            if x == NX - 1:
                xp = xp + highest[0] * m
            zm, zp = ends(here, edge(press_item, 0, x, zpairs) + zfill, 1)
            for c, (a, b) in enumerate(((xm, xp), (ym, yp), (zm, zp))):
                r = res[flat(c * NX + x)] - 0.5 * (b - a)
                res[flat(c * NX + x)] = r
                put(fine, c * NX + x, inverse * r)

        def during(stage):
            if stage == 0:
                acc = jnp.zeros((NY, NZ), jnp.float32)
                for p in range(3 * NX):
                    acc = acc + adj[flat(p)] * res[flat(p)]
                put_sum(acc)
                ar_start(0, turn)
            elif stage == 1:
                ar_finish(0, turn)
                ar_start(1, turn)
            elif stage == 2:
                ar_finish(1, turn)
                ar_start(2, turn)

        cycle(3, during, False)
        divergence(lambda: None, False)
        return carry

    lax.fori_loop(1, SCHUR_ITERS, iteration, 0)

    ar_finish(2, SCHUR_ITERS - 1)
    add_mean()
    m8 = mean[1]
    m = jnp.concatenate([m8, m8], axis=0)
    for x in range(NX):
        out_p[x] = get(press, x) - m
        for c in range(3):
            out_v[c, x] = get(vel, c * NX + x)
        out_t[x] = out_t[x] + RAYLEIGH * get(vel, 2 * NX + x)


def solution(mesh):
    sizes = tuple(mesh.shape[a] for a in AXES)

    def shards(heat, motion, dual, rheology, stiffness):
        cells = heat.size * sizes[0] * sizes[1] * sizes[2]
        vmem = pl.BlockSpec(memory_space=pltpu.VMEM)
        f32 = jnp.float32
        padded = lambda planes: pltpu.VMEM((FIRST + planes * PITCH, NZ), f32)
        flat = lambda planes: pltpu.VMEM((planes * NY, NZ), f32)
        slots = sum(n - 1 for n in sizes)
        return pl.pallas_call(
            functools.partial(kernel, sizes, cells),
            out_shape=(
                jax.ShapeDtypeStruct(heat.shape, f32),
                jax.ShapeDtypeStruct(motion.shape, f32),
                jax.ShapeDtypeStruct(heat.shape, f32),
            ),
            in_specs=[vmem] * 4 + [pl.BlockSpec(memory_space=pltpu.SMEM)],
            out_specs=(vmem,) * 3,
            scratch_shapes=[
                padded(6 * NX), padded(6 * CX), padded(3 * NX), padded(NX), padded(2 * NX), padded(CX),
                flat(6 * NX), flat(3 * NX), flat(3 * NX), flat(3 * NX), flat(6 * CX), padded(2 * NX),
                pltpu.VMEM((7, NX * NY, NZ), f32), pltpu.VMEM((7, CX * NY, NZ), f32), pltpu.VMEM((7, NX * NY, NZ), f32),
                pltpu.VMEM((6, NX * NY, NZ), f32),
                pltpu.VMEM((ROUNDS, 2, 6 * NY, NZ), f32), pltpu.VMEM((ROUNDS, 2, 6 * NY, NZ), f32),
                pltpu.VMEM((ROUNDS, 2, 6 * NX, NZ), f32), pltpu.VMEM((ROUNDS, 2, 6 * NX, NZ), f32),
                pltpu.VMEM((ROUNDS, NY, NZ), f32), pltpu.VMEM((ROUNDS, 2, NY, NZ), f32),
                pltpu.VMEM((8, NZ), f32), pltpu.VMEM((2, 8, NZ), f32),
                pltpu.VMEM((SCHUR_ITERS, 3, 8, NZ), f32), pltpu.VMEM((SCHUR_ITERS, slots, 8, NZ), f32),
                pltpu.SemaphoreType.DMA((ROUNDS, 6)), pltpu.SemaphoreType.DMA((ROUNDS, 6)),
                pltpu.SemaphoreType.DMA((SCHUR_ITERS, slots)), pltpu.SemaphoreType.DMA((SCHUR_ITERS, slots)),
            ],
            compiler_params=pltpu.CompilerParams(collective_id=0, has_side_effects=True),
        )(heat, motion, dual, rheology, stiffness)

    return jax.shard_map(
        shards,
        mesh=mesh,
        in_specs=(P(*AXES), P(None, *AXES), P(*AXES), P(*AXES), P()),
        out_specs=(P(*AXES), P(None, *AXES), P(*AXES)),
        check_vma=False,
    )
```

time: 899 us -> 115 us (0.13); the launches traced: 885 us -> 115 us
  starting transfers between devices: 468 us -> 0 us
  blocking collectives: 185 us -> 0 us
  Pallas kernels: 0 us -> 110 us
  waiting for transfers between devices: 95.9 us -> 0 us
  local copies, waits for them, and re-layouts: 81 us -> 3.75 us
  other arithmetic: 47.3 us -> 0 us
    ppermute x162 -> x0, starting transfers between devices: 468 us -> none  [the longest x81 334 us: extended(): lax.ppermute(last, axis, up)]
    psum x16 -> x0, blocking collectives: 185 us -> none  [by_axis(): value = lax.psum(value, axis)]
    pallas_call x0 -> x1, Pallas kernels: none -> 110 us  [shards(): pl.pallas_call(functools.partial(kernel, sizes, cells), out_shape=(jax.Sh...]
    ppermute x162 -> x0, waiting for transfers between devices: 95.9 us -> none  [the longest x81 53.9 us: extended(): lax.ppermute(initial, axis, [(b, a) for a, b in up])]
    reshape x13 -> x0, local copies, waits for them, and re-layouts: 66.8 us -> none  [the longest x5 61.2 us: restrict(): field.reshape(leading + (cells_x // 2, 2, cells_y // 2, 2, cells_z // 2, 2))]
    reduce_sum x9 -> x0, other arithmetic: 27.6 us -> none  [the longest x5 24.6 us: restrict(): return blocks.mean(axis=(-5, -3, -1))]
  transfers between devices with their start and end apart: 162 -> 0, of which waited for: 41 -> 0; matrix products, arithmetic and copies ran while one was open for 1% -> 0% of each run, Pallas kernels for 0% -> 0%
where the time goes in v1:
time: 115 us
  Pallas kernels  110 us (96%)
  local copies, waits for them, and re-layouts  3.75 us (3%)
    pallas_call x1, Pallas kernels, shards(): pl.pallas_call(functools.partial(kernel, sizes, cells), out_shape=(jax.Sh...  110 us
    unnamed x5, local copies, waits for them, and re-layouts  3.75 us

profile of v1, /device:TPU:1, one launch (start us, length us, event | category | flops | bytes accessed | tf_op | source)
XLA Modules:
  0.0 114.9 jit_solution(14258524168902765409)
XLA Ops:
  0.6 110.5 %shard_map.76 = (f32[8,16,128]{2,1,0:T(8,128)}, f32[3,8,16,128]{3,2,1,0:T(8,128)}, f32[8,16,128]{2,1,0:T(8,128)}) custom-call(f32[8,16,128]{2,1,0:T(8,128)} %heat.1, f32[3,8,16,128]{3,2,1,0:T(8,128)} %motion.1, f32[8,16,128]{2,1,0:T(8,128)} %dual.1, s32[8,16,128]{2,1,0:T(8,128)} %rheology.1, f32[8]{0:T(128)} %stiffness.1), custom_call_target="tpu_custom_call" | custom-call | tf_op jit(solution)/shard_map/pallas_call | solution.py:519
  111.1 1.5 %copy.11 = f32[8,16,128]{2,1,0:T(8,128)} copy(f32[8,16,128]{2,1,0:T(8,128)} %get-tuple-element.6) | data formatting | bytes 131072
  112.6 0.0 copy-start
  112.6 1.6 %copy.12 = f32[3,8,16,128]{3,2,1,0:T(8,128)} copy(f32[3,8,16,128]{3,2,1,0:T(8,128)} %get-tuple-element.7) | data formatting | bytes 393216
  114.3 0.0 copy-done
  114.3 0.6 copy.13
Async XLA Ops:
  112.6 1.7 %copy-start = (f32[8,16,128]{2,1,0:T(8,128)S(1)}, f32[8,16,128]{2,1,0:T(8,128)}, u32[]{:S(2)}) copy-start(f32[8,16,128]{2,1,0:T(8,128)} %get-tuple-element.8) | copy-start | bytes 196612

commit v2 on v1

--- a/solution.py
+++ b/solution.py
@@ -26,8 +26,15 @@
 FIRST = 8
 KEEP = 1.0 - JACOBI_WEIGHT
 
-HEAT1, HEAT2, FIELDS, PRESSURE, FIRST_SMOOTH, SWEEP1, SWEEP2, LAST_SMOOTH, VELOCITY = range(9)
-ROUNDS = 9
+HEAT1, HEAT2, FIELDS, PRESSURE, FIRST_SMOOTH, VELOCITY = range(6)
+ROUNDS = 6
+
+CY, CZ = NY // 2, NZ // 2
+DEPTH = COARSE_SWEEPS
+EX = CX + 2 * DEPTH
+ER = 16
+COARSE_VISC, COARSE_ITERATE = range(2)
+AROUND = [(dx, dy, dz) for dx in (-1, 0, 1) for dy in (-1, 0, 1) for dz in (-1, 0, 1) if (dx, dy, dz) != (0, 0, 0)]
 
 
 def row(plane):
@@ -46,15 +53,34 @@
         return self.lane + (c * self.planes + x) * 2 * self.width
 
 
-def kernel(sizes, total_cells, heat, motion, dual, rheology, stiffness, out_t, out_v, out_p, fine, coarse, vel, press,
-           fields, cvisc, res, src, adj, held, cres, trans, kf, kc, kh, aux, xs, xr, ys, yr, zs, zr, psum, mean, ar_out,
-           ar_in, send_sem, recv_sem, ar_send, ar_recv):
+def kernel(sizes, total_cells, heat, motion, dual, rheology, stiffness, out_t, out_v, out_p, fine, vel, press,
+           fields, res, src, adj, held, trans, kf, kc, kh, aux, xs, xr, ys, yr, zs, zr, psum, mean, ar_out, ar_in,
+           own, wide, swept, halves, grown, grown_ends, cinv, cxs, cys, czs, czys, cxr, cyr, cxyr, czr, czyr, zq,
+           send_sem, recv_sem, ar_send, ar_recv, c_send, c_recv):
     at = [lax.axis_index(a) for a in AXES]
     barrier = pltpu.get_barrier_semaphore()
     peers = sum(n - 1 for n in sizes)
     for axis, me, n in zip(AXES, at, sizes):
         for d in range(1, n):
             pl.semaphore_signal(barrier, inc=1, device_id={axis: lax.rem(me + d, n)}, device_id_type=MESH)
+
+    def there(d):
+        ok = None
+        for me, n, step in zip(at, sizes, d):
+            if step:
+                inside = me < n - 1 if step > 0 else me > 0
+                ok = inside if ok is None else jnp.logical_and(ok, inside)
+        return ok
+
+    def device(d):
+        return {axis: lax.rem(me + n + step, n) for axis, me, n, step in zip(AXES, at, sizes, d)}
+
+    for d in AROUND:
+        if sum(map(abs, d)) > 1:
+            @pl.when(there(d))
+            def _():
+                pl.semaphore_signal(barrier, inc=1, device_id=device(d), device_id_type=MESH)
+            peers = peers + there(d).astype(jnp.int32)
 
     lanes = lax.broadcasted_iota(jnp.int32, (NY, NZ), 1)
     rows = lax.broadcasted_iota(jnp.int32, (NY, NZ), 0)
@@ -166,11 +192,131 @@
     def flat(plane):
         return slice(plane * NY, (plane + 1) * NY)
 
-    def restrict_pair(a, b):
-        s = a + b
-        s = s + jnp.where(even_row, pltpu.roll(s, NY - 1, 0), pltpu.roll(s, 1, 0))
-        s = s + jnp.where(even_lane, lroll(s, -1), lroll(s, 1))
-        return 0.125 * s
+    lanes8 = lax.broadcasted_iota(jnp.int32, (CY, NZ), 1)
+    left8 = lanes8 < CZ
+    left = lanes < CZ
+    left4 = lax.broadcasted_iota(jnp.int32, (4, NZ), 1) < CZ
+    squeeze = 2 * (lanes8 & (CZ - 1))
+    repeat = lanes >> 1
+    outer = jnp.where(lanes == 0, NZ - 1, CZ)
+    beyond = jnp.where(lanes >= NZ - DEPTH, lanes - (NZ - DEPTH), (lanes - CZ + DEPTH) & 7)
+
+    def take(v, index):
+        return jnp.take_along_axis(v, index, axis=1)
+
+    def tile(p):
+        return slice(p * CY, (p + 1) * CY)
+
+    def restrict(slot, a, b):
+        r = slot * NY
+        halves[r:r + NY] = a + b
+        t = halves[pl.ds(r, CY, stride=2), :] + halves[pl.ds(r + 1, CY, stride=2), :]
+        return take(t + lroll(t, -1), squeeze) * 0.125
+
+    def c_copies(t, nc):
+        xr_n, yr_n, z_n = (3 * nc + 1) // 2 * CY, 8 * nc, (CX * nc + 15) // 16 * CY
+        out = []
+        for i, d in enumerate(AROUND):
+            dx, dy, dz = d
+            hx, hy, hz = (dx < 0) * 1, (dy < 0) * 1, (dz < 0) * 1
+            if dz:
+                if dy:
+                    source = czys.at[t, hy, pl.ds(0, z_n // 2)]
+                    target = czyr.at[t, dx + 1, hy, hz, pl.ds(0, z_n // 2)]
+                else:
+                    source, target = czs.at[t, pl.ds(0, z_n)], czr.at[t, dx + 1, hz, pl.ds(0, z_n)]
+            elif dx and dy:
+                source = cys.at[t, hy, pl.ds(0 if dx < 0 else 4 * nc, 4 * nc)]
+                target = cxyr.at[t, hx, hy, pl.ds(0, 4 * nc)]
+            elif dy:
+                source, target = cys.at[t, hy, pl.ds(0, yr_n)], cyr.at[t, hy, pl.ds(0, yr_n)]
+            else:
+                source, target = cxs.at[t, hx, pl.ds(0, xr_n)], cxr.at[t, hx, pl.ds(0, xr_n)]
+            copy = pltpu.make_async_remote_copy(
+                src_ref=source, dst_ref=target, send_sem=c_send.at[t, i], recv_sem=c_recv.at[t, i],
+                device_id=device(d), device_id_type=MESH)
+            out.append((copy, there(d), there(tuple(-v for v in d))))
+        return out
+
+    def c_start(t, nc):
+        for h, first in ((0, 1), (1, 0)):
+            for q in range((3 * nc + 1) // 2):
+                a, b = first * nc + 2 * q, first * nc + min(2 * q + 1, 3 * nc - 1)
+                cxs[t, h, tile(q)] = jnp.where(left8, own[tile(a)], own[tile(b)])
+            rows_from = 4 if h == 0 else 0
+            for q in range(2 * nc):
+                a, b = 2 * q * CY + rows_from, (2 * q + 1) * CY + rows_from
+                cys[t, h, 4 * q:4 * q + 4] = jnp.where(left4, own[a:a + 4], own[b:b + 4])
+        for part in range((CX * nc + 15) // 16):
+            acc = jnp.zeros((CY, NZ), jnp.float32)
+            for g in range(16 * part, min(16 * part + 16, CX * nc)):
+                spot = g % 16 * 8
+                acc = jnp.where((lanes8 >> 3) == g % 16, lroll(own[tile(g)], spot - (CZ - DEPTH)), acc)
+            czs[t, tile(part)] = acc
+            czys[t, 0, 4 * part:4 * part + 4] = acc[4:8]
+            czys[t, 1, 4 * part:4 * part + 4] = acc[0:4]
+        for copy, sends, _ in c_copies(t, nc):
+            pl.when(sends)(copy.start)
+
+    def c_finish(t, nc):
+        for copy, _, gets in c_copies(t, nc):
+            pl.when(gets)(copy.wait_recv)
+        for copy, sends, _ in c_copies(t, nc):
+            pl.when(sends)(copy.wait_send)
+
+    def wide_row(c, e):
+        return FIRST + (c * EX + e) * ER
+
+    def assemble(t, nc):
+        group = (lanes8 & 7) < DEPTH
+        group4 = (lax.broadcasted_iota(jnp.int32, (4, NZ), 1) & 7) < DEPTH
+        for dx in range(3):
+            for part in range((CX * nc + 15) // 16):
+                r = (dx * 2 + part) * ER
+                zq[r + 4:r + 12] = jnp.where(group, czr[t, dx, 0, tile(part)], czr[t, dx, 1, tile(part)])
+                for h, at_row in ((0, 0), (1, 12)):
+                    four = slice(4 * part, 4 * part + 4)
+                    zq[r + at_row:r + at_row + 4] = jnp.where(group4, czyr[t, dx, h, 0, four], czyr[t, dx, h, 1, four])
+        for c in range(nc):
+            for e in range(EX):
+                x = e - DEPTH
+                r = wide_row(c, e)
+                if 0 <= x < CX:
+                    dx, sender = 0, x
+                elif x < 0:
+                    dx, sender = -1, x + CX
+                else:
+                    dx, sender = 1, x - CX
+                p = sender * nc + c
+                if dx == 0:
+                    wide[r + 4:r + 12] = own[tile(p)]
+                else:
+                    i = p - (nc if dx < 0 else 0)
+                    v = cxr[t, 0 if dx < 0 else 1, tile(i // 2)]
+                    wide[r + 4:r + 12] = v if i % 2 == 0 else lroll(v, CZ)
+                if -DEPTH < x < CX + DEPTH - 1:
+                    q = p // 2
+                    for h, at_row in ((0, 0), (1, 12)):
+                        if dx == 0:
+                            v = cyr[t, h, 4 * q:4 * q + 4]
+                        else:
+                            k = 4 * (q - (nc if dx < 0 else 0))
+                            v = cxyr[t, 0 if dx < 0 else 1, h, k:k + 4]
+                        wide[r + at_row:r + at_row + 4] = v if p % 2 == 0 else lroll(v, CZ)
+                    g = p
+                    z = zq[((dx_from(dx)) * 2 + g // 16) * ER:((dx_from(dx)) * 2 + g // 16) * ER + ER]
+                    wide[r:r + ER] = jnp.where(left, wide[r:r + ER], take(z, (beyond + g % 16 * 8) & (NZ - 1)))
+
+    def dx_from(dx):
+        return 1 - dx
+
+    def sweep(source, target, c, e, keep):
+        r = wide_row(c, e)
+        k = [kc[n, e * ER:(e + 1) * ER] for n in range(6)]
+        here = source[r:r + ER]
+        total = keep * here + k[0] * source[r - ER:r] + k[1] * source[r + ER:r + 2 * ER]
+        total = total + k[2] * source[r - 1:r - 1 + ER] + k[3] * source[r + 1:r + 1 + ER]
+        return total + k[4] * lroll(here, 1) + k[5] * lroll(here, -1)
 
     order = (1, 2, 0)
     base_slot = {}
@@ -223,6 +369,25 @@
                     into = (xr, yr, zr)[k]
                     into[t, s] = jnp.zeros(into.shape[2:], jnp.float32)
 
+    for d in AROUND:
+        @pl.when(jnp.logical_not(there(tuple(-v for v in d))))
+        def _():
+            dx, dy, dz = d
+            hx, hy, hz = (dx < 0) * 1, (dy < 0) * 1, (dz < 0) * 1
+            for t in range(2):
+                if dz and dy:
+                    into = czyr.at[t, dx + 1, hy, hz]
+                elif dz:
+                    into = czr.at[t, dx + 1, hz]
+                elif dx and dy:
+                    into = cxyr.at[t, hx, hy]
+                elif dy:
+                    into = cyr.at[t, hy]
+                else:
+                    into = cxr.at[t, hx]
+                into[...] = jnp.zeros(into.shape, jnp.float32)
+
+    wide[...] = jnp.zeros_like(wide)
     mean[...] = jnp.zeros_like(mean)
     heat_item = Item(fields, 1, NX, 1)
     trans_item = Item(trans, 1, NX, 1, xoff=NY, yoff=NX, lane=2 * NX)
@@ -305,15 +470,14 @@
         put(fields, x, stepped[x])
         put(fields, NX + x, aux[1, flat(x)] * jnp.exp(-ACTIVATION_ENERGY * stepped[x]))
     for x in range(CX):
-        put(cvisc, x, restrict_pair(get(fields, NX + 2 * x), get(fields, NX + 2 * x + 1)))
+        own[tile(x)] = restrict(x, get(fields, NX + 2 * x), get(fields, NX + 2 * x + 1))
     both = Item(fields, 2, NX, 1)
-    cv_item = Item(cvisc, 1, CX, 2, xoff=2 * NY, yoff=2 * NX, lane=64)
-    pack(FIELDS, [both, cv_item])
-    start(FIELDS, 3 * NY, 2 * NX + 8)
-    finish(FIELDS, 3 * NY, 2 * NX + 8)
+    c_start(COARSE_VISC, 1)
+    pack(FIELDS, [both])
+    start(FIELDS, 2 * NY, 2 * NX)
+    finish(FIELDS, 2 * NY, 2 * NX)
 
     zpairs = unpack(FIELDS, both)
-    cpairs = unpack(FIELDS, cv_item)
     for x in range(NX):
         here, xm, xp, ym, yp = sides(FIELDS, both, 0, x)
         zm, zp = ends(here, edge(both, 0, x, zpairs), 1)
@@ -336,23 +500,40 @@
             res[flat(k * NX + x)] = s
             put(fine, (3 + k) * NX + x, inverse * g)
             put(fine, k * NX + x, inverse * s)
-    for x in range(CX):
-        here, xm, xp, ym, yp = sides(FIELDS, cv_item, 0, x)
-        zm, zp = ends(here, edge(cv_item, 0, x, cpairs), 2)
-        six = [0.125 * (here + v) for v in (xm, xp, ym, yp, zm, zp)]
-        set_coefs(kc, x, six, 2)
-        aux[5, flat(x)] = JACOBI_WEIGHT / ((six[0] + six[1]) + (six[2] + six[3]) + (six[4] + six[5]))
+    c_finish(COARSE_VISC, 1)
+    assemble(COARSE_VISC, 1)
+    inside_rows = jnp.logical_and(jnp.logical_or(rows >= 4, at[1] > 0), jnp.logical_or(rows < 12, at[1] < sizes[1] - 1))
+    inside = jnp.logical_or(left, jnp.logical_or(
+        jnp.logical_and(lanes >= NZ - DEPTH, at[2] > 0),
+        jnp.logical_and(lanes < CZ + DEPTH, at[2] < sizes[2] - 1)))
+    inside = jnp.logical_and(inside, inside_rows)
+    for e in range(1, EX - 1):
+        r = wide_row(0, e)
+        here = wide[r:r + ER]
+        others = (wide[r - ER:r], wide[r + ER:r + 2 * ER], wide[r - 1:r - 1 + ER], wide[r + 1:r + 1 + ER],
+                  lroll(here, 1), lroll(here, -1))
+        six = [0.125 * (here + v) for v in others]
+        ok = inside
+        if e < DEPTH:
+            ok = jnp.logical_and(ok, at[0] > 0)
+        elif e >= DEPTH + CX:
+            ok = jnp.logical_and(ok, at[0] < sizes[0] - 1)
+        inverse = jnp.where(ok, JACOBI_WEIGHT / ((six[0] + six[1]) + (six[2] + six[3]) + (six[4] + six[5])), 0.0)
+        for n in range(6):
+            kc[n, e * ER:(e + 1) * ER] = jnp.where(ok, inverse * six[n], 0.0)
+        if DEPTH <= e < DEPTH + CX:
+            grown[0:ER] = inverse
+            cinv[tile(e - DEPTH)] = take(grown[4:12], lanes8 & (CZ - 1))
 
     def cycle(nc, during, first):
-        fi, ci = Item(fine, nc, NX, 1), Item(coarse, nc, CX, 2)
-        fx, fy, cx, cy = nc * NY, nc * NX, nc * NY, (nc * CX + 7) // 8 * 8
+        fi = Item(fine, nc, NX, 1)
+        fx, fy = nc * NY, nc * NX
         pack(FIRST_SMOOTH, [fi])
         start(FIRST_SMOOTH, fx, fy)
         during(0)
         finish(FIRST_SMOOTH, fx, fy)
         zpairs = unpack(FIRST_SMOOTH, fi)
         for x in range(CX):
-            inv_c = aux[5, flat(x)]
             ka, kb = coefs(kf, 2 * x), coefs(kf, 2 * x + 1)
             for c in range(nc):
                 pa, pb = c * NX + 2 * x, c * NX + 2 * x + 1
@@ -361,48 +542,57 @@
                 if first and c >= 3:
                     held[flat(pa - 3 * NX)] = a
                     held[flat(pb - 3 * NX)] = b
-                r = restrict_pair(a, b)
-                cres[flat(c * CX + x)] = r
-                put(coarse, c * CX + x, inv_c * r)
-        for sweep in range(COARSE_SWEEPS - 1):
-            t = SWEEP1 + sweep
-            pack(t, [ci])
-            start(t, cx, cy)
-            during(1 + sweep)
-            finish(t, cx, cy)
-            cpairs = unpack(t, ci)
-            last = sweep == COARSE_SWEEPS - 2
-            swept = []
-            for x in range(CX):
-                inv_c = aux[5, flat(x)]
-                k = coefs(kc, x)
-                for c in range(nc):
-                    total, here = gather(t, ci, c, x, k, cpairs)
-                    e = KEEP * here + inv_c * (cres[flat(c * CX + x)] + total)
-                    if last:
-                        for q in (2 * x, 2 * x + 1):
-                            put(fine, c * NX + q, get(fine, c * NX + q) + e)
-                    else:
-                        swept.append((c * CX + x, e))
-            for plane, e in swept:
-                put(coarse, plane, e)
-        pack(LAST_SMOOTH, [fi])
-        start(LAST_SMOOTH, fx, fy)
-        during(3)
-        finish(LAST_SMOOTH, fx, fy)
-        zpairs = unpack(LAST_SMOOTH, fi)
+                own[tile(x * nc + c)] = cinv[tile(x)] * restrict(x * nc + c, a, b)
+        c_start(COARSE_ITERATE, nc)
+        during(1)
+        c_finish(COARSE_ITERATE, nc)
+        assemble(COARSE_ITERATE, nc)
+        for e in range(1, EX - 1):
+            for c in range(nc):
+                r = wide_row(c, e)
+                swept[r:r + ER] = sweep(wide, swept, c, e, 2.0 - JACOBI_WEIGHT)
+        for e in range(2, EX - 2):
+            for c in range(nc):
+                r = wide_row(c, e)
+                v = wide[r:r + ER] + sweep(swept, None, c, e, KEEP)
+                base = (c * 6 + e - 2) * 2 * ER
+                full = take(v, repeat)
+                for k in (0, 8):
+                    for odd in (0, 1):
+                        grown[pl.ds(base + 2 * k + odd, 8, stride=2), :] = full[k:k + 8]
+                if DEPTH <= e < DEPTH + CX:
+                    base = (c * CX + e - DEPTH) * 2 * ER
+                    full = take(v, outer)
+                    for k in (0, 8):
+                        for odd in (0, 1):
+                            grown_ends[pl.ds(base + 2 * k + odd, 8, stride=2), :] = full[k:k + 8]
+
+        acc = jnp.zeros((NY, NZ), jnp.float32)
         for x in range(NX):
             k = coefs(kf, x)
             inverse = aux[3, flat(x)]
             for c in range(nc):
-                total, here = gather(LAST_SMOOTH, fi, c, x, k, zpairs)
-                new = KEEP * here + inverse * (res[flat(c * NX + x)] + total)
+                here, xm, xp, ym, yp = sides(FIRST_SMOOTH, fi, c, x)
+                base = [(c * 6 + q // 2 + 1) * 2 * ER + FIRST for q in (x - 1, x, x + 1)]
+                whole = here + grown[base[1]:base[1] + NY]
+                total = k[0] * (xm + grown[base[0]:base[0] + NY]) + k[1] * (xp + grown[base[2]:base[2] + NY])
+                total = total + k[2] * (ym + grown[base[1] - 1:base[1] - 1 + NY])
+                total = total + k[3] * (yp + grown[base[1] + 1:base[1] + 1 + NY])
+                at_edge = (c * CX + x // 2) * 2 * ER + FIRST
+                total = total + k[4] * lroll(whole, 1) + k[5] * lroll(whole, -1)
+                total = total + k[6] * (edge(fi, c, x, zpairs) + grown_ends[at_edge:at_edge + NY])
+                new = KEEP * whole + here + inverse * total
                 if c >= 3:
                     adj[flat((c - 3) * NX + x)] = new
                 elif first:
                     put(vel, c * NX + x, new)
+                    p = c * NX + x
+                    acc = acc + held[flat(p)] * whole + get(fine, 3 * NX + p) * res[flat(p)]
                 else:
                     put(vel, c * NX + x, get(vel, c * NX + x) + new)
+        if first:
+            put_sum(acc)
+            ar_start(0, 0)
 
     vel_item, press_item = Item(vel, 3, NX, 1), Item(press, 1, NX, 1)
 
@@ -420,19 +610,7 @@
             change = aux[4, flat(x)] * ((xp - xm) + (yp - ym) + (zp - zm))
             put(press, x, -change if first else get(press, x) - change)
 
-    def first_during(stage):
-        if stage == 3:
-            acc = jnp.zeros((NY, NZ), jnp.float32)
-            for x in range(NX):
-                inverse = aux[3, flat(x)]
-                for c in range(3):
-                    p = c * NX + x
-                    acc = acc + held[flat(p)] * get(fine, p)
-                    acc = acc + (inverse * res[flat(3 * NX + p)]) * res[flat(p)]
-            put_sum(acc)
-            ar_start(0, 0)
-
-    cycle(6, first_during, True)
+    cycle(6, lambda stage: None, True)
 
     def first_sum():
         ar_finish(0, 0)
@@ -485,12 +663,14 @@
             elif stage == 1:
                 ar_finish(0, turn)
                 ar_start(1, turn)
-            elif stage == 2:
-                ar_finish(1, turn)
-                ar_start(2, turn)
 
         cycle(3, during, False)
-        divergence(lambda: None, False)
+
+        def last_stage():
+            ar_finish(1, turn)
+            ar_start(2, turn)
+
+        divergence(last_stage, False)
         return carry
 
     lax.fori_loop(1, SCHUR_ITERS, iteration, 0)
@@ -526,17 +706,27 @@
             in_specs=[vmem] * 4 + [pl.BlockSpec(memory_space=pltpu.SMEM)],
             out_specs=(vmem,) * 3,
             scratch_shapes=[
-                padded(6 * NX), padded(6 * CX), padded(3 * NX), padded(NX), padded(2 * NX), padded(CX),
-                flat(6 * NX), flat(3 * NX), flat(3 * NX), flat(3 * NX), flat(6 * CX), padded(2 * NX),
-                pltpu.VMEM((7, NX * NY, NZ), f32), pltpu.VMEM((7, CX * NY, NZ), f32), pltpu.VMEM((7, NX * NY, NZ), f32),
-                pltpu.VMEM((6, NX * NY, NZ), f32),
+                padded(6 * NX), padded(3 * NX), padded(NX), padded(2 * NX),
+                flat(6 * NX), flat(3 * NX), flat(3 * NX), flat(3 * NX), padded(2 * NX),
+                pltpu.VMEM((7, NX * NY, NZ), f32), pltpu.VMEM((6, EX * ER, NZ), f32), pltpu.VMEM((7, NX * NY, NZ), f32),
+                pltpu.VMEM((5, NX * NY, NZ), f32),
                 pltpu.VMEM((ROUNDS, 2, 6 * NY, NZ), f32), pltpu.VMEM((ROUNDS, 2, 6 * NY, NZ), f32),
                 pltpu.VMEM((ROUNDS, 2, 6 * NX, NZ), f32), pltpu.VMEM((ROUNDS, 2, 6 * NX, NZ), f32),
                 pltpu.VMEM((ROUNDS, NY, NZ), f32), pltpu.VMEM((ROUNDS, 2, NY, NZ), f32),
                 pltpu.VMEM((8, NZ), f32), pltpu.VMEM((2, 8, NZ), f32),
                 pltpu.VMEM((SCHUR_ITERS, 3, 8, NZ), f32), pltpu.VMEM((SCHUR_ITERS, slots, 8, NZ), f32),
+                pltpu.VMEM((6 * CX * CY, NZ), f32), pltpu.VMEM((2 * FIRST + 6 * EX * ER, NZ), f32),
+                pltpu.VMEM((2 * FIRST + 6 * EX * ER, NZ), f32), pltpu.VMEM((6 * CX * NY, NZ), f32),
+                pltpu.VMEM((6 * 6 * 2 * ER, NZ), f32), pltpu.VMEM((6 * CX * 2 * ER, NZ), f32),
+                pltpu.VMEM((CX * CY, NZ), f32),
+                pltpu.VMEM((2, 2, 9 * CY, NZ), f32), pltpu.VMEM((2, 2, 48, NZ), f32),
+                pltpu.VMEM((2, 16, NZ), f32), pltpu.VMEM((2, 2, 8, NZ), f32),
+                pltpu.VMEM((2, 2, 9 * CY, NZ), f32), pltpu.VMEM((2, 2, 48, NZ), f32),
+                pltpu.VMEM((2, 2, 2, 24, NZ), f32), pltpu.VMEM((2, 3, 2, 16, NZ), f32),
+                pltpu.VMEM((2, 3, 2, 2, 8, NZ), f32), pltpu.VMEM((3 * 2 * ER, NZ), f32),
                 pltpu.SemaphoreType.DMA((ROUNDS, 6)), pltpu.SemaphoreType.DMA((ROUNDS, 6)),
                 pltpu.SemaphoreType.DMA((SCHUR_ITERS, slots)), pltpu.SemaphoreType.DMA((SCHUR_ITERS, slots)),
+                pltpu.SemaphoreType.DMA((2, 26)), pltpu.SemaphoreType.DMA((2, 26)),
             ],
             compiler_params=pltpu.CompilerParams(collective_id=0, has_side_effects=True),
         )(heat, motion, dual, rheology, stiffness)

time: 115 us -> 102 us (0.89)
  Pallas kernels: 110 us -> 97.7 us
    pallas_call x1, Pallas kernels: 110 us -> 97.7 us  [shards(): pl.pallas_call(functools.partial(kernel, sizes, cells), out_shape=(jax.Sh...]
where the time goes in v2:
time: 102 us
  Pallas kernels  97.7 us (96%)
  local copies, waits for them, and re-layouts  3.75 us (4%)
    pallas_call x1, Pallas kernels, shards(): pl.pallas_call(functools.partial(kernel, sizes, cells), out_shape=(jax.Sh...  97.7 us
    unnamed x5, local copies, waits for them, and re-layouts  3.75 us

profile of v2, /device:TPU:1, one launch (start us, length us, event | category | flops | bytes accessed | tf_op | source)
XLA Modules:
  0.0 102.1 jit_solution(3997594306517993672)
XLA Ops:
  0.6 97.7 %shard_map.76 = (f32[8,16,128]{2,1,0:T(8,128)}, f32[3,8,16,128]{3,2,1,0:T(8,128)}, f32[8,16,128]{2,1,0:T(8,128)}) custom-call(f32[8,16,128]{2,1,0:T(8,128)} %heat.1, f32[3,8,16,128]{3,2,1,0:T(8,128)} %motion.1, f32[8,16,128]{2,1,0:T(8,128)} %dual.1, s32[8,16,128]{2,1,0:T(8,128)} %rheology.1, f32[8]{0:T(128)} %stiffness.1), custom_call_target="tpu_custom_call" | custom-call | tf_op jit(solution)/shard_map/pallas_call | solution.py:699
  98.4 1.5 %copy.11 = f32[8,16,128]{2,1,0:T(8,128)} copy(f32[8,16,128]{2,1,0:T(8,128)} %get-tuple-element.6) | data formatting | bytes 131072
  99.8 0.0 copy-start
  99.8 1.6 %copy.12 = f32[3,8,16,128]{3,2,1,0:T(8,128)} copy(f32[3,8,16,128]{3,2,1,0:T(8,128)} %get-tuple-element.7) | data formatting | bytes 393216
  101.5 0.0 copy-done
  101.5 0.6 copy.13
Async XLA Ops:
  99.8 1.7 %copy-start = (f32[8,16,128]{2,1,0:T(8,128)S(1)}, f32[8,16,128]{2,1,0:T(8,128)}, u32[]{:S(2)}) copy-start(f32[8,16,128]{2,1,0:T(8,128)} %get-tuple-element.8) | copy-start | bytes 196612

commit v3 on v2

--- a/solution.py
+++ b/solution.py
@@ -34,7 +34,8 @@
 EX = CX + 2 * DEPTH
 ER = 16
 COARSE_VISC, COARSE_ITERATE = range(2)
-AROUND = [(dx, dy, dz) for dx in (-1, 0, 1) for dy in (-1, 0, 1) for dz in (-1, 0, 1) if (dx, dy, dz) != (0, 0, 0)]
+AROUND = [(dx, dy, dz) for dx in (-1, 1, 0) for dz in (-1, 1, 0) for dy in (-1, 1, 0) if (dx, dy, dz) != (0, 0, 0)]
+ENDS_FIRST = (0, NX - 1) + tuple(range(1, NX - 1))
 
 
 def row(plane):
@@ -53,34 +54,39 @@
         return self.lane + (c * self.planes + x) * 2 * self.width
 
 
-def kernel(sizes, total_cells, heat, motion, dual, rheology, stiffness, out_t, out_v, out_p, fine, vel, press,
-           fields, res, src, adj, held, trans, kf, kc, kh, aux, xs, xr, ys, yr, zs, zr, psum, mean, ar_out, ar_in,
+def kernel(sizes, total_cells, heat, motion, dual, rheology, stiffness, out_t, out_v, out_p, out_m, fine, vel, press,
+           fields, res, src, adj, held, sums, trans, kf, kc, kh, aux, xs, xr, ys, yr, zs, zr, psum, mean, ar_out, ar_in,
            own, wide, swept, halves, grown, grown_ends, cinv, cxs, cys, czs, czys, cxr, cyr, cxyr, czr, czyr, zq,
            send_sem, recv_sem, ar_send, ar_recv, c_send, c_recv):
     at = [lax.axis_index(a) for a in AXES]
     barrier = pltpu.get_barrier_semaphore()
-    peers = sum(n - 1 for n in sizes)
-    for axis, me, n in zip(AXES, at, sizes):
-        for d in range(1, n):
-            pl.semaphore_signal(barrier, inc=1, device_id={axis: lax.rem(me + d, n)}, device_id_type=MESH)
+    after = [lax.rem(me + 1, n) for me, n in zip(at, sizes)]
+    before = [lax.rem(me + n - 1, n) for me, n in zip(at, sizes)]
+    up, down = [me < n - 1 for me, n in zip(at, sizes)], [me > 0 for me in at]
 
     def there(d):
         ok = None
-        for me, n, step in zip(at, sizes, d):
+        for k, step in enumerate(d):
             if step:
-                inside = me < n - 1 if step > 0 else me > 0
+                inside = up[k] if step > 0 else down[k]
                 ok = inside if ok is None else jnp.logical_and(ok, inside)
         return ok
 
-    def device(d):
-        return {axis: lax.rem(me + n + step, n) for axis, me, n, step in zip(AXES, at, sizes, d)}
-
+    exists = {d: there(d) for d in AROUND}
+    beside = {d: {axis: after[k] if d[k] > 0 else before[k] for k, axis in enumerate(AXES) if d[k]} for d in AROUND}
+    line = []
+    for axis, me, n in zip(AXES, at, sizes):
+        line.append([{axis: lax.rem(me + d, n)} for d in range(1, n)])
+    peers = sum(n - 1 for n in sizes)
+    for others in line:
+        for other in others:
+            pl.semaphore_signal(barrier, inc=1, device_id=other, device_id_type=MESH)
     for d in AROUND:
         if sum(map(abs, d)) > 1:
-            @pl.when(there(d))
+            @pl.when(exists[d])
             def _():
-                pl.semaphore_signal(barrier, inc=1, device_id=device(d), device_id_type=MESH)
-            peers = peers + there(d).astype(jnp.int32)
+                pl.semaphore_signal(barrier, inc=1, device_id=beside[d], device_id_type=MESH)
+            peers = peers + exists[d].astype(jnp.int32)
 
     lanes = lax.broadcasted_iota(jnp.int32, (NY, NZ), 1)
     rows = lax.broadcasted_iota(jnp.int32, (NY, NZ), 0)
@@ -94,28 +100,29 @@
     def lroll(v, shift):
         return pltpu.roll(v, shift % NZ, 1)
 
-    def copies(t, xrows, yrows):
+    def copies(t, xrows, yrows, axes):
         out = []
-        for k, (axis, me, n) in enumerate(zip(AXES, at, sizes)):
+        for k in axes:
             for s in (0, 1):
                 source = (xs.at[t, s, pl.ds(0, xrows)], ys.at[t, s, pl.ds(0, yrows)], zs.at[t])[k]
                 target = (xr.at[t, s, pl.ds(0, xrows)], yr.at[t, s, pl.ds(0, yrows)], zr.at[t, s])[k]
-                peer = lax.rem(me + (1 if s == 0 else n - 1), n)
+                step = 1 if s == 0 else -1
+                d = tuple(step if axis == k else 0 for axis in range(3))
+                opposite = tuple(-v for v in d)
                 copy = pltpu.make_async_remote_copy(
                     src_ref=source, dst_ref=target, send_sem=send_sem.at[t, 2 * k + s],
-                    recv_sem=recv_sem.at[t, 2 * k + s], device_id={axis: peer}, device_id_type=MESH)
-                up, down = me < n - 1, me > 0
-                out.append((copy, up if s == 0 else down, down if s == 0 else up))
+                    recv_sem=recv_sem.at[t, 2 * k + s], device_id=beside[d], device_id_type=MESH)
+                out.append((copy, exists[d], exists[opposite]))
         return out
 
-    def start(t, xrows, yrows):
-        for copy, sends, _ in copies(t, xrows, yrows):
+    def start(t, xrows, yrows, axes):
+        for copy, sends, _ in copies(t, xrows, yrows, axes):
             pl.when(sends)(copy.start)
 
     def finish(t, xrows, yrows):
-        for copy, _, gets in copies(t, xrows, yrows):
+        for copy, _, gets in copies(t, xrows, yrows, (1, 2, 0)):
             pl.when(gets)(copy.wait_recv)
-        for copy, sends, _ in copies(t, xrows, yrows):
+        for copy, sends, _ in copies(t, xrows, yrows, (1, 2, 0)):
             pl.when(sends)(copy.wait_send)
 
     def pack_lanes(acc, value, spot, w):
@@ -124,23 +131,33 @@
     def chunks(n):
         return [(a, min(8, n - a)) for a in range(0, n, 8)]
 
-    def pack(t, items):
-        acc = jnp.zeros((NY, NZ), jnp.float32)
+    def extent(items):
+        return sum(it.comps for it in items) * NY, sum(it.count() for it in items)
+
+    def send_x(t, items):
         for it in items:
             for c in range(it.comps):
                 p = (it.first + c) * it.planes
                 at_row = it.xoff + c * NY
                 xs[t, 0, at_row:at_row + NY] = it.ref[row(p + it.planes - 1):row(p + it.planes - 1) + NY]
                 xs[t, 1, at_row:at_row + NY] = it.ref[row(p):row(p) + NY]
-            base = row(it.first * it.planes)
-            for a, size in chunks(it.count()):
-                ys[t, 0, it.yoff + a:it.yoff + a + size] = it.ref[pl.ds(base + a * PITCH + NY - 1, size, stride=PITCH), :]
-                ys[t, 1, it.yoff + a:it.yoff + a + size] = it.ref[pl.ds(base + a * PITCH, size, stride=PITCH), :]
+        start(t, *extent(items), (0,))
+
+    def send_yz(t, items):
+        acc = jnp.zeros((NY, NZ), jnp.float32)
+        for it in items:
             for c in range(it.comps):
                 for x in range(it.planes):
                     r = row((it.first + c) * it.planes + x)
                     acc = pack_lanes(acc, it.ref[r:r + NY], it.spot(c, x), it.width)
         zs[t] = acc
+        start(t, *extent(items), (2,))
+        for it in items:
+            base = row(it.first * it.planes)
+            for a, size in chunks(it.count()):
+                ys[t, 0, it.yoff + a:it.yoff + a + size] = it.ref[pl.ds(base + a * PITCH + NY - 1, size, stride=PITCH), :]
+                ys[t, 1, it.yoff + a:it.yoff + a + size] = it.ref[pl.ds(base + a * PITCH, size, stride=PITCH), :]
+        start(t, *extent(items), (1,))
 
     def unpack(t, it, low_extra=None, high_extra=None):
         base = row(it.first * it.planes)
@@ -234,19 +251,11 @@
                 source, target = cxs.at[t, hx, pl.ds(0, xr_n)], cxr.at[t, hx, pl.ds(0, xr_n)]
             copy = pltpu.make_async_remote_copy(
                 src_ref=source, dst_ref=target, send_sem=c_send.at[t, i], recv_sem=c_recv.at[t, i],
-                device_id=device(d), device_id_type=MESH)
-            out.append((copy, there(d), there(tuple(-v for v in d))))
+                device_id=beside[d], device_id_type=MESH)
+            out.append((copy, exists[d], exists[tuple(-v for v in d)]))
         return out
 
     def c_start(t, nc):
-        for h, first in ((0, 1), (1, 0)):
-            for q in range((3 * nc + 1) // 2):
-                a, b = first * nc + 2 * q, first * nc + min(2 * q + 1, 3 * nc - 1)
-                cxs[t, h, tile(q)] = jnp.where(left8, own[tile(a)], own[tile(b)])
-            rows_from = 4 if h == 0 else 0
-            for q in range(2 * nc):
-                a, b = 2 * q * CY + rows_from, (2 * q + 1) * CY + rows_from
-                cys[t, h, 4 * q:4 * q + 4] = jnp.where(left4, own[a:a + 4], own[b:b + 4])
         for part in range((CX * nc + 15) // 16):
             acc = jnp.zeros((CY, NZ), jnp.float32)
             for g in range(16 * part, min(16 * part + 16, CX * nc)):
@@ -255,8 +264,23 @@
             czs[t, tile(part)] = acc
             czys[t, 0, 4 * part:4 * part + 4] = acc[4:8]
             czys[t, 1, 4 * part:4 * part + 4] = acc[0:4]
-        for copy, sends, _ in c_copies(t, nc):
-            pl.when(sends)(copy.start)
+        copies26 = c_copies(t, nc)
+        def go(kind):
+            for d, (copy, sends, _) in zip(AROUND, copies26):
+                if kind(d):
+                    pl.when(sends)(copy.start)
+        go(lambda d: d[0] and d[2])
+        for h, first in ((0, 1), (1, 0)):
+            for q in range((3 * nc + 1) // 2):
+                a, b = first * nc + 2 * q, first * nc + min(2 * q + 1, 3 * nc - 1)
+                cxs[t, h, tile(q)] = jnp.where(left8, own[tile(a)], own[tile(b)])
+        go(lambda d: d == (1, 0, 0) or d == (-1, 0, 0))
+        for h, rows_from in ((0, 4), (1, 0)):
+            for q in range(2 * nc):
+                a, b = 2 * q * CY + rows_from, (2 * q + 1) * CY + rows_from
+                cys[t, h, 4 * q:4 * q + 4] = jnp.where(left4, own[a:a + 4], own[b:b + 4])
+        go(lambda d: d[0] and d[1] and not d[2])
+        go(lambda d: not d[0])
 
     def c_finish(t, nc):
         for copy, _, gets in c_copies(t, nc):
@@ -326,14 +350,14 @@
         slots += sizes[axis] - 1
 
     def ar_copies(axis, turn):
-        n, me = sizes[axis], at[axis]
+        n = sizes[axis]
         out = []
         for d in range(1, n):
             slot = base_slot[axis] + d - 1
             out.append(pltpu.make_async_remote_copy(
                 src_ref=ar_out.at[turn, order.index(axis)], dst_ref=ar_in.at[turn, slot],
                 send_sem=ar_send.at[turn, slot], recv_sem=ar_recv.at[turn, slot],
-                device_id={AXES[axis]: lax.rem(me + d, n)}, device_id_type=MESH))
+                device_id=line[axis][d - 1], device_id_type=MESH))
         return out
 
     def ar_start(stage, turn):
@@ -370,7 +394,7 @@
                     into[t, s] = jnp.zeros(into.shape[2:], jnp.float32)
 
     for d in AROUND:
-        @pl.when(jnp.logical_not(there(tuple(-v for v in d))))
+        @pl.when(jnp.logical_not(exists[tuple(-v for v in d)]))
         def _():
             dx, dy, dz = d
             hx, hy, hz = (dx < 0) * 1, (dy < 0) * 1, (dz < 0) * 1
@@ -424,7 +448,7 @@
         acc = pack_lanes(acc, jnp.where(low[1], am * lam, ap * lam), trans_item.spot(0, x), 1)
     zs[HEAT1] = acc
     pl.semaphore_wait(barrier, peers)
-    start(HEAT1, 2 * NY, 2 * NX)
+    start(HEAT1, 2 * NY, 2 * NX, (0, 2, 1))
     for x in range(NX):
         base = jnp.zeros((NY, NZ), jnp.float32)
         for layer in range(LAYERS):
@@ -433,18 +457,16 @@
     finish(HEAT1, 2 * NY, 2 * NX)
 
     zpairs = unpack(HEAT1, heat_item)
-    stepped = []
-    for x in range(NX):
+    next_item = Item(fields, 1, NX, 1, first=2)
+    for x in ENDS_FIRST:
         total, here = gather(HEAT1, heat_item, 0, x, coefs(kh, x), zpairs)
-        stepped.append(aux[0, flat(x)] * here + total)
-    for x in range(NX):
-        put(fields, x, stepped[x])
-    pack(HEAT2, [heat_item])
-    start(HEAT2, NY, NX)
-
-    for a in (0,):
-        trans[pl.ds(row(0) - 1, NX, stride=PITCH), :] = yr[HEAT1, 0, NX:2 * NX]
-        trans[pl.ds(row(NX) + NY, NX, stride=PITCH), :] = yr[HEAT1, 1, NX:2 * NX]
+        put(fields, 2 * NX + x, aux[0, flat(x)] * here + total)
+        if x == NX - 1:
+            send_x(HEAT2, [next_item])
+    send_yz(HEAT2, [next_item])
+
+    trans[pl.ds(row(0) - 1, NX, stride=PITCH), :] = yr[HEAT1, 0, NX:2 * NX]
+    trans[pl.ds(row(NX) + NY, NX, stride=PITCH), :] = yr[HEAT1, 1, NX:2 * NX]
     for x in range(NX):
         lam = dual[x]
         ap_x = lambda i: (spread - step * jnp.minimum(motion[0, i], 0.0)) * dual[i]
@@ -461,24 +483,24 @@
         out_t[x] = total
     finish(HEAT2, NY, NX)
 
-    zpairs = unpack(HEAT2, heat_item)
-    stepped = []
-    for x in range(NX):
-        total, here = gather(HEAT2, heat_item, 0, x, coefs(kh, x), zpairs)
-        stepped.append(aux[0, flat(x)] * here + total)
-    for x in range(NX):
-        put(fields, x, stepped[x])
-        put(fields, NX + x, aux[1, flat(x)] * jnp.exp(-ACTIVATION_ENERGY * stepped[x]))
+    zpairs = unpack(HEAT2, next_item)
+    both = Item(fields, 2, NX, 1)
+    for x in ENDS_FIRST:
+        total, here = gather(HEAT2, next_item, 0, x, coefs(kh, x), zpairs)
+        t2 = aux[0, flat(x)] * here + total
+        put(fields, x, t2)
+        put(fields, NX + x, aux[1, flat(x)] * jnp.exp(-ACTIVATION_ENERGY * t2))
+        if x == NX - 1:
+            send_x(FIELDS, [both])
     for x in range(CX):
         own[tile(x)] = restrict(x, get(fields, NX + 2 * x), get(fields, NX + 2 * x + 1))
-    both = Item(fields, 2, NX, 1)
     c_start(COARSE_VISC, 1)
-    pack(FIELDS, [both])
-    start(FIELDS, 2 * NY, 2 * NX)
+    send_yz(FIELDS, [both])
     finish(FIELDS, 2 * NY, 2 * NX)
 
     zpairs = unpack(FIELDS, both)
-    for x in range(NX):
+    six_item = Item(fine, 6, NX, 1)
+    for x in ENDS_FIRST:
         here, xm, xp, ym, yp = sides(FIELDS, both, 0, x)
         zm, zp = ends(here, edge(both, 0, x, zpairs), 1)
         lam = -INCREMENT_DT * dual[x]
@@ -500,6 +522,9 @@
             res[flat(k * NX + x)] = s
             put(fine, (3 + k) * NX + x, inverse * g)
             put(fine, k * NX + x, inverse * s)
+        if x == NX - 1:
+            send_x(FIRST_SMOOTH, [six_item])
+    send_yz(FIRST_SMOOTH, [six_item])
     c_finish(COARSE_VISC, 1)
     assemble(COARSE_VISC, 1)
     inside_rows = jnp.logical_and(jnp.logical_or(rows >= 4, at[1] > 0), jnp.logical_or(rows < 12, at[1] < sizes[1] - 1))
@@ -525,11 +550,11 @@
             grown[0:ER] = inverse
             cinv[tile(e - DEPTH)] = take(grown[4:12], lanes8 & (CZ - 1))
 
+    vel_item, press_item = Item(vel, 3, NX, 1), Item(press, 1, NX, 1)
+
     def cycle(nc, during, first):
         fi = Item(fine, nc, NX, 1)
         fx, fy = nc * NY, nc * NX
-        pack(FIRST_SMOOTH, [fi])
-        start(FIRST_SMOOTH, fx, fy)
         during(0)
         finish(FIRST_SMOOTH, fx, fy)
         zpairs = unpack(FIRST_SMOOTH, fi)
@@ -537,14 +562,32 @@
             ka, kb = coefs(kf, 2 * x), coefs(kf, 2 * x + 1)
             for c in range(nc):
                 pa, pb = c * NX + 2 * x, c * NX + 2 * x + 1
-                a = KEEP * res[flat(pa)] + gather(FIRST_SMOOTH, fi, c, 2 * x, ka, zpairs)[0]
-                b = KEEP * res[flat(pb)] + gather(FIRST_SMOOTH, fi, c, 2 * x + 1, kb, zpairs)[0]
+                a = gather(FIRST_SMOOTH, fi, c, 2 * x, ka, zpairs)[0]
+                b = gather(FIRST_SMOOTH, fi, c, 2 * x + 1, kb, zpairs)[0]
+                sums[flat(pa)] = a
+                sums[flat(pb)] = b
+                a = KEEP * res[flat(pa)] + a
+                b = KEEP * res[flat(pb)] + b
                 if first and c >= 3:
                     held[flat(pa - 3 * NX)] = a
                     held[flat(pb - 3 * NX)] = b
                 own[tile(x * nc + c)] = cinv[tile(x)] * restrict(x * nc + c, a, b)
         c_start(COARSE_ITERATE, nc)
         during(1)
+        acc = jnp.zeros((NY, NZ), jnp.float32)
+        for x in range(NX):
+            inverse = aux[3, flat(x)]
+            for c in range(nc):
+                p = c * NX + x
+                here = get(fine, p)
+                part = (1.0 + KEEP) * here + inverse * sums[flat(p)]
+                if c >= 3:
+                    adj[flat(p - 3 * NX)] = part
+                elif first:
+                    put(vel, p, part)
+                    acc = acc + held[flat(p)] * here + get(fine, 3 * NX + p) * res[flat(p)]
+                else:
+                    put(vel, p, get(vel, p) + part)
         c_finish(COARSE_ITERATE, nc)
         assemble(COARSE_ITERATE, nc)
         for e in range(1, EX - 1):
@@ -567,48 +610,46 @@
                         for odd in (0, 1):
                             grown_ends[pl.ds(base + 2 * k + odd, 8, stride=2), :] = full[k:k + 8]
 
-        acc = jnp.zeros((NY, NZ), jnp.float32)
-        for x in range(NX):
+        if first:
+            for x in range(NX):
+                for c in range(3):
+                    base = (c * 6 + x // 2 + 1) * 2 * ER + FIRST
+                    acc = acc + held[flat(c * NX + x)] * grown[base:base + NY]
+            put_sum(acc)
+            ar_start(0, 0)
+        for x in ENDS_FIRST:
             k = coefs(kf, x)
             inverse = aux[3, flat(x)]
             for c in range(nc):
-                here, xm, xp, ym, yp = sides(FIRST_SMOOTH, fi, c, x)
                 base = [(c * 6 + q // 2 + 1) * 2 * ER + FIRST for q in (x - 1, x, x + 1)]
-                whole = here + grown[base[1]:base[1] + NY]
-                total = k[0] * (xm + grown[base[0]:base[0] + NY]) + k[1] * (xp + grown[base[2]:base[2] + NY])
-                total = total + k[2] * (ym + grown[base[1] - 1:base[1] - 1 + NY])
-                total = total + k[3] * (yp + grown[base[1] + 1:base[1] + 1 + NY])
+                here = grown[base[1]:base[1] + NY]
+                total = k[0] * grown[base[0]:base[0] + NY] + k[1] * grown[base[2]:base[2] + NY]
+                total = total + k[2] * grown[base[1] - 1:base[1] - 1 + NY] + k[3] * grown[base[1] + 1:base[1] + 1 + NY]
                 at_edge = (c * CX + x // 2) * 2 * ER + FIRST
-                total = total + k[4] * lroll(whole, 1) + k[5] * lroll(whole, -1)
-                total = total + k[6] * (edge(fi, c, x, zpairs) + grown_ends[at_edge:at_edge + NY])
-                new = KEEP * whole + here + inverse * total
+                total = total + (k[4] * lroll(here, 1) + k[5] * lroll(here, -1)) + k[6] * grown_ends[at_edge:at_edge + NY]
+                part = KEEP * here + inverse * total
+                p = c * NX + x
                 if c >= 3:
-                    adj[flat((c - 3) * NX + x)] = new
-                elif first:
-                    put(vel, c * NX + x, new)
-                    p = c * NX + x
-                    acc = acc + held[flat(p)] * whole + get(fine, 3 * NX + p) * res[flat(p)]
+                    adj[flat(p - 3 * NX)] = adj[flat(p - 3 * NX)] + part
                 else:
-                    put(vel, c * NX + x, get(vel, c * NX + x) + new)
-        if first:
-            put_sum(acc)
-            ar_start(0, 0)
-
-    vel_item, press_item = Item(vel, 3, NX, 1), Item(press, 1, NX, 1)
-
-    def divergence(during, first):
-        pack(VELOCITY, [vel_item])
-        start(VELOCITY, 3 * NY, 3 * NX)
+                    put(vel, p, get(vel, p) + part)
+            if x == NX - 1:
+                send_x(VELOCITY, [vel_item])
+        send_yz(VELOCITY, [vel_item])
+
+    def divergence(during, first, send):
         during()
         finish(VELOCITY, 3 * NY, 3 * NX)
         zpairs = unpack(VELOCITY, vel_item)
-        for x in range(NX):
+        for x in ENDS_FIRST:
             _, xm, xp, _, _ = sides(VELOCITY, vel_item, 0, x)
             _, _, _, ym, yp = sides(VELOCITY, vel_item, 1, x)
             here = get(vel, 2 * NX + x)
             zm, zp = ends(here, edge(vel_item, 2, x, zpairs), 1)
             change = aux[4, flat(x)] * ((xp - xm) + (yp - ym) + (zp - zm))
             put(press, x, -change if first else get(press, x) - change)
+            if x == NX - 1 and send is not None:
+                send()
 
     cycle(6, lambda stage: None, True)
 
@@ -616,7 +657,11 @@
         ar_finish(0, 0)
         ar_start(1, 0)
 
-    divergence(first_sum, True)
+    def send_pressure():
+        send_x(PRESSURE, [press_item])
+
+    divergence(first_sum, True, send_pressure)
+    send_yz(PRESSURE, [press_item])
     ar_finish(1, 0)
     ar_start(2, 0)
 
@@ -624,8 +669,6 @@
     highest = [jnp.where(me == n - 1, 1.0, 0.0) for me, n in zip(at, sizes)]
 
     def iteration(turn, carry):
-        pack(PRESSURE, [press_item])
-        start(PRESSURE, NY, NX)
         zpairs = jnp.where(upper[1], lroll(zr[VELOCITY, 0], 1), lroll(zr[VELOCITY, 1], -1))
         for x in range(NX):
             k = coefs(kf, x)
@@ -640,7 +683,8 @@
         m = jnp.concatenate([m8, m8], axis=0)
         zpairs = unpack(PRESSURE, press_item, lowest[1] * m8, highest[1] * m8)
         zfill = jnp.where(low[1], lowest[2], highest[2]) * m
-        for x in range(NX):
+        three = Item(fine, 3, NX, 1)
+        for x in ENDS_FIRST:
             inverse = aux[3, flat(x)]
             here, xm, xp, ym, yp = sides(PRESSURE, press_item, 0, x)
             if x == 0:
@@ -652,6 +696,9 @@
                 r = res[flat(c * NX + x)] - 0.5 * (b - a)
                 res[flat(c * NX + x)] = r
                 put(fine, c * NX + x, inverse * r)
+            if x == NX - 1:
+                send_x(FIRST_SMOOTH, [three])
+        send_yz(FIRST_SMOOTH, [three])
 
         def during(stage):
             if stage == 0:
@@ -670,20 +717,30 @@
             ar_finish(1, turn)
             ar_start(2, turn)
 
-        divergence(last_stage, False)
+        not_last = turn < SCHUR_ITERS - 1
+        divergence(last_stage, False, lambda: pl.when(not_last)(send_pressure))
+
+        @pl.when(not_last)
+        def _():
+            send_yz(PRESSURE, [press_item])
         return carry
 
     lax.fori_loop(1, SCHUR_ITERS, iteration, 0)
 
     ar_finish(2, SCHUR_ITERS - 1)
     add_mean()
-    m8 = mean[1]
-    m = jnp.concatenate([m8, m8], axis=0)
+    out_m[...] = mean[1]
     for x in range(NX):
-        out_p[x] = get(press, x) - m
+        out_p[x] = get(press, x)
         for c in range(3):
             out_v[c, x] = get(vel, c * NX + x)
-        out_t[x] = out_t[x] + RAYLEIGH * get(vel, 2 * NX + x)
+
+
+def outputs(transported, velocity, pressure, mean, out_t, out_v, out_p):
+    out_t[...] = transported[...] + RAYLEIGH * velocity[2]
+    out_v[...] = velocity[...]
+    m = mean[...]
+    out_p[...] = pressure[...] - jnp.concatenate([m, m], axis=0)[None]
 
 
 def solution(mesh):
@@ -696,18 +753,19 @@
         padded = lambda planes: pltpu.VMEM((FIRST + planes * PITCH, NZ), f32)
         flat = lambda planes: pltpu.VMEM((planes * NY, NZ), f32)
         slots = sum(n - 1 for n in sizes)
-        return pl.pallas_call(
+        found = (
+            jax.ShapeDtypeStruct(heat.shape, f32),
+            jax.ShapeDtypeStruct(motion.shape, f32),
+            jax.ShapeDtypeStruct(heat.shape, f32),
+        )
+        parts = pl.pallas_call(
             functools.partial(kernel, sizes, cells),
-            out_shape=(
-                jax.ShapeDtypeStruct(heat.shape, f32),
-                jax.ShapeDtypeStruct(motion.shape, f32),
-                jax.ShapeDtypeStruct(heat.shape, f32),
-            ),
+            out_shape=found + (jax.ShapeDtypeStruct((8, NZ), f32),),
             in_specs=[vmem] * 4 + [pl.BlockSpec(memory_space=pltpu.SMEM)],
-            out_specs=(vmem,) * 3,
+            out_specs=(vmem,) * 4,
             scratch_shapes=[
-                padded(6 * NX), padded(3 * NX), padded(NX), padded(2 * NX),
-                flat(6 * NX), flat(3 * NX), flat(3 * NX), flat(3 * NX), padded(2 * NX),
+                padded(6 * NX), padded(3 * NX), padded(NX), padded(3 * NX),
+                flat(6 * NX), flat(3 * NX), flat(3 * NX), flat(3 * NX), flat(6 * NX), padded(2 * NX),
                 pltpu.VMEM((7, NX * NY, NZ), f32), pltpu.VMEM((6, EX * ER, NZ), f32), pltpu.VMEM((7, NX * NY, NZ), f32),
                 pltpu.VMEM((5, NX * NY, NZ), f32),
                 pltpu.VMEM((ROUNDS, 2, 6 * NY, NZ), f32), pltpu.VMEM((ROUNDS, 2, 6 * NY, NZ), f32),
@@ -730,6 +788,7 @@
             ],
             compiler_params=pltpu.CompilerParams(collective_id=0, has_side_effects=True),
         )(heat, motion, dual, rheology, stiffness)
+        return pl.pallas_call(outputs, out_shape=found, in_specs=[vmem] * 4, out_specs=(vmem,) * 3)(*parts)
 
     return jax.shard_map(
         shards,

time: 102 us -> 95.8 us (0.939)
  local copies, waits for them, and re-layouts: 3.75 us -> 0 us
  Pallas kernels: 97.7 us -> 95 us
    unnamed x5 -> x0, local copies, waits for them, and re-layouts: 3.75 us -> none
    pallas_call x1 -> x2, Pallas kernels: 97.7 us -> 95 us  [the longest x1 93.3 us: shards(): pl.pallas_call(functools.partial(kernel, sizes, cells), out_shape=found +...]
where the time goes in v3:
time: 95.8 us; the launch traced here: 95.7 us
  Pallas kernels  95 us (99%)
    pallas_call x1, Pallas kernels, shards(): pl.pallas_call(functools.partial(kernel, sizes, cells), out_shape=found +...  93.3 us

profile of v3, /device:TPU:1, one launch (start us, length us, event | category | flops | bytes accessed | tf_op | source)
XLA Modules:
  0.0 95.7 jit_solution(16113670372030746181)
XLA Ops:
  0.6 93.3 %shard_map.76 = (f32[8,16,128]{2,1,0:T(8,128)}, f32[3,8,16,128]{3,2,1,0:T(8,128)}, f32[8,16,128]{2,1,0:T(8,128)}, f32[8,128]{1,0:T(8,128)}) custom-call(f32[8,16,128]{2,1,0:T(8,128)} %heat.1, f32[3,8,16,128]{3,2,1,0:T(8,128)} %motion.1, f32[8,16,128]{2,1,0:T(8,128)} %dual.1, s32[8,16,128]{2,1,0:T(8,128)} %rheology.1, f32[8]{0:T(128)} %stiffness.1), custom_call_target="tpu_custom_call" | custom-call | tf_op jit(solution)/shard_map/pallas_call | solution.py:761
  94.0 1.7 %shard_map.77 = (f32[8,16,128]{2,1,0:T(8,128)}, f32[3,8,16,128]{3,2,1,0:T(8,128)}, f32[8,16,128]{2,1,0:T(8,128)}) custom-call(f32[8,16,128]{2,1,0:T(8,128)} %get-tuple-element.7.transported, f32[3,8,16,128]{3,2,1,0:T(8,128)} %get-tuple-element.8.velocity, f32[8,16,128]{2,1,0:T(8,128)} %get-tuple-element.9.pressure, f32[8,128]{1,0:T(8,128)} %get-tuple-element.10.mean), custom_call_target="tpu_custom_call" | custom-call | tf_op jit(solution)/shard_map/pallas_call | solution.py:791
